TPU v7x, 32 devices: a whole 2x2x4 slice. The times are simulated.
32 devices in a mesh: branch: 2 (over x), strip: 16 (over z, y, core).
Axes of the slice: x: 2, y: 2, z: 4, core: 2. Of those that a mesh axis runs over, the one named last changes fastest.
Arguments:
- image_feats: bfloat16 [32, 2048, 256], P(None, ('branch', 'strip')), may hold values from -6 to 6
- cam_weights: bfloat16 [3, 9, 256, 256], replicated, may hold values from -0.1875 to 0.1875
- depth_weight: bfloat16 [256, 118], replicated, may hold values from -1.5 to 1.5
- ray_bins: int32 [2048, 118], P(('branch', 'strip')), may hold values from 0 to 2047, as said below
- pillar_sums: bfloat16 [32, 256, 128], P(None, ('branch', 'strip')), may hold values from -12 to 12
- pillar_counts: int32 [32, 256], P(None, ('branch', 'strip')), may hold values from 0 to 8
- lidar_weight: bfloat16 [4, 128, 128], replicated, may hold values from -0.375 to 0.375
- merge_weight: bfloat16 [9, 384, 256], replicated, may hold values from -0.15625 to 0.15625
- out_cotangent: bfloat16 [16, 128, 256], P(None, ('branch', 'strip')), may hold values from -6 to 6
Outputs:
- merged: bfloat16 [16, 128, 256], P(None, ('branch', 'strip'))
- cam_grad: bfloat16 [32, 2048, 256], P(None, ('branch', 'strip'))
- lid_grad: bfloat16 [16, 128, 128], P(None, ('branch', 'strip'))
Inputs may be any that keep to these rules, and one draw needn't show every extreme that they name: For a column j of sector s = j // 64, ray_bins[j, k] lies in sector s - 1, s or s + 1 taken modulo 32, in cycle k * 16 // 118.
All inputs are finite; a program needn't handle non-finite values.
Results may differ from a plain program's by a relative error of at most 0.014.
Values may be sent and summed in bfloat16 or wider, within the bound.
A program may use at most 128 MiB of HBM per device.

v0:
```python
import functools

import jax
import jax.numpy as jnp
from jax import lax
from jax.experimental import pallas as pl
from jax.experimental.pallas import tpu as pltpu
from jax.sharding import PartitionSpec as P

AXES = ("branch", "strip")
CH = 8
BLOCK = 16


def rolled_sum(low, mid, high, period):
    rows = mid.shape[0]
    place = lax.broadcasted_iota(jnp.int32, mid.shape, 0) & (period - 1)
    down = jnp.where(place == 0, 0.0, pltpu.roll(low, 1, 0))
    up = jnp.where(place == period - 1, 0.0, pltpu.roll(high, rows - 1, 0))
    return mid + down + up


def conv_rows(src, pieces, weights, layer, height):
    taps = [
        jnp.concatenate([src[pl.ds(s + i * height, rows), :] for s, rows in pieces], axis=0)
        for i in range(3)
    ]
    x = jnp.concatenate(taps, axis=1)
    channels = taps[0].shape[1]
    z = [
        jnp.dot(
            x,
            weights[layer, 3 * dy : 3 * dy + 3].reshape(3 * channels, -1),
            preferred_element_type=jnp.float32,
        )
        for dy in range(3)
    ]
    total = rolled_sum(z[0], z[1], z[2], height)
    return jnp.maximum(total, 0.0).astype(jnp.bfloat16)


def one_hot_rows(rows, sources, source_of):
    p = lax.broadcasted_iota(jnp.int32, (rows, sources), 0)
    q = lax.broadcasted_iota(jnp.int32, (rows, sources), 1)
    return jnp.where(source_of(p) == q, 1.0, 0.0).astype(jnp.bfloat16)


def row_numbers(shape):
    return lax.broadcasted_iota(jnp.int32, shape, 0).astype(jnp.float32).astype(jnp.bfloat16)


def pick_of(row_id, codes, j):
    groups, lanes = row_id.shape
    code = jnp.broadcast_to(codes[pl.ds(j, 1), :], (16, lanes)).astype(jnp.bfloat16)
    code = jnp.concatenate([code] * (groups // 16), axis=0)
    one, zero = jnp.ones((), jnp.bfloat16), jnp.zeros((), jnp.bfloat16)
    return jnp.where(row_id[...] == code, one, zero)


def block_turn():
    shift = BLOCK.bit_length() - 1
    return one_hot_rows(
        BLOCK * BLOCK,
        BLOCK * BLOCK,
        lambda p: ((p & (BLOCK - 1)) << shift) + (p >> shift),
    )


def kernel(
    n, strips, cols, height, br, ba, bins_n,
    img_hbm, cw_hbm, wd, bins, pillars, counts, lw, cot, mw_hbm,
    merged_o, lidgrad_o, table, codes, feats_o, amat_o, probs_o, slope_o,
    img, cw, mw, xin, y1, y2, feats, wdp, probs, slope, sums, low, row_id, amat, parts, sendbuf,
    rp1, rp2, rp3, rm1, rm2, rm3, win, lidwin, cotwin,
    local_sem, out_sem, send_sem, recv_sem,
):
    me = lax.axis_index(AXES[0]) * strips + lax.axis_index(AXES[1])
    ch_rows = CH * height
    lanes = wdp.shape[0]

    def dev(d):
        t = lax.rem(me + d + n, n)
        return (t // strips, t % strips)

    barrier = pltpu.get_barrier_semaphore()
    for d in (1, 2, 3, -1, -2, -3):
        pl.semaphore_signal(
            barrier, inc=1, device_id=dev(d), device_id_type=pl.DeviceIdType.MESH
        )
    layers = cw.shape[0]
    image = pltpu.make_async_copy(img_hbm, img, local_sem.at[layers + 1])
    image.start()
    fetches = [
        pltpu.make_async_copy(cw_hbm.at[k], cw.at[k], local_sem.at[k]) for k in range(layers)
    ]
    fetches.append(pltpu.make_async_copy(mw_hbm, mw, local_sem.at[layers]))
    for copy in fetches:
        copy.start()

    sec = ba * br
    cot_own, lid_own = (ba + 1) * br, (ba + 2) * br
    cot_f = cot[...].astype(jnp.float32)
    for a in range(ba):
        cotwin[pl.ds(cot_own + a * br, br), :] = cot_f[:, a, :].astype(jnp.bfloat16)
    points = counts[...]
    scale = (points > 0).astype(jnp.float32) / jnp.maximum(points, 1).astype(jnp.float32)
    pil = pillars[...].astype(jnp.float32)
    pil = jnp.concatenate(
        [pil[k] * scale[:, k : k + 1] for k in range(2 * br)], axis=0
    ).astype(jnp.bfloat16)
    lb, la = br.bit_length() - 1, ba.bit_length() - 1

    def pillar_row(p):
        r, a, uv = p & (br - 1), (p >> lb) & (ba - 1), p >> (lb + la)
        return ((2 * r + (uv >> 1)) << (la + 1)) + 2 * a + (uv & 1)

    gathered = jnp.dot(
        one_hot_rows(4 * sec, 4 * sec, pillar_row), pil, preferred_element_type=jnp.float32
    ).astype(jnp.bfloat16)
    taps = jnp.concatenate([gathered[k * sec : (k + 1) * sec] for k in range(4)], axis=1)
    lid = jnp.dot(
        taps, lw[...].reshape(taps.shape[1], -1), preferred_element_type=jnp.float32
    )
    lidwin[pl.ds(lid_own, sec), :] = jnp.maximum(lid, 0.0).astype(jnp.bfloat16)

    cell = br * ba
    sh_cell, sh_ba, sh_br = cell.bit_length() - 1, ba.bit_length() - 1, br.bit_length() - 1
    raw = bins[...]
    off = (raw >> sh_cell) - me + 1
    off = jnp.where(off < 0, off + n, off)
    off = jnp.where(off >= n, off - n, off)
    in_cell = raw & (cell - 1)
    code = (((off << sh_ba) + (in_cell & (ba - 1))) << sh_br) + (in_cell >> sh_ba)
    codes[...] = jnp.full(codes.shape, -1.0, jnp.float32)
    codes[:, 0:bins_n] = code.astype(jnp.float32)
    row_id[...] = row_numbers(row_id.shape)
    wdp[...] = jnp.zeros_like(wdp)
    wdp[0:bins_n, :] = wd[...]
    parts[...] = jnp.zeros_like(parts)
    image.wait()
    turn = block_turn()
    for j0 in range(0, cols, BLOCK):
        for h0 in range(0, height, BLOCK):
            block = img[h0 : h0 + BLOCK, j0 : j0 + BLOCK, :].reshape(BLOCK * BLOCK, -1)
            turned = jnp.dot(turn, block, preferred_element_type=jnp.float32)
            turned = turned.astype(jnp.bfloat16)
            for c in range(BLOCK):
                at = (3 + j0 + c) * height + h0
                xin[pl.ds(at, BLOCK), :] = turned[c * BLOCK : (c + 1) * BLOCK]
    fetches[0].wait()

    def interior(src, dst, layer, first, shift, count, wide):
        def step(i, carry):
            c = jnp.minimum(first + wide * i, cols - first - wide) + shift
            at = pl.multiple_of(c * height, height)
            size = wide * height
            dst[pl.ds(at, size), :] = conv_rows(src, [(at, size)], cw, layer, height)
            return carry

        lax.fori_loop(0, count, step, 0)

    full = cols // CH
    interior(xin, y1, 0, 1, 2, full // 2, 2 * CH)
    pl.semaphore_wait(barrier, 6)

    messages = []

    def send(src, dst, d):
        m = len(messages)
        copy = pltpu.make_async_remote_copy(
            src_ref=src,
            dst_ref=dst,
            send_sem=send_sem.at[m],
            recv_sem=recv_sem.at[m],
            device_id=dev(d),
            device_id_type=pl.DeviceIdType.MESH,
        )
        copy.start()
        messages.append(copy)

    h3 = 3 * height
    send(xin.at[pl.ds(cols * height, h3)], xin.at[pl.ds(0, h3)], 1)
    send(xin.at[pl.ds(h3, h3)], xin.at[pl.ds((cols + 3) * height, h3)], -1)
    for window, start, edge in ((cotwin, cot_own, br), (lidwin, lid_own, 2 * br)):
        mine = window.at[pl.ds(start, sec)]
        send(mine, window.at[pl.ds(edge, sec)], 1)
        send(mine, window.at[pl.ds(start + sec, sec)], -1)
        last = window.at[pl.ds(start + sec - edge, edge)]
        send(last, window.at[pl.ds(0, edge)], 2)
        send(window.at[pl.ds(start, edge)], window.at[pl.ds(start + 2 * sec, edge)], -2)

    fetches[1].wait()
    interior(y1, y2, 1, 2, 1, full // 2, 2 * CH)
    fetches[2].wait()
    interior(y2, feats, 2, 3, 0, full // 2 - 1, 2 * CH)

    messages[0].wait_recv()
    messages[1].wait_recv()
    for layer, (src, dst, extra, done) in enumerate(
        ((xin, y1, 4, cols - 2), (y1, y2, 2, cols - 4), (y2, feats, 0, cols - 2 * CH))
    ):
        right = (3 + done) * height
        size = (cols + extra) * height - right
        edge = conv_rows(src, [(0, h3), (right, size)], cw, layer, height)
        dst[pl.ds(0, h3), :] = edge[:h3]
        dst[pl.ds(right, size), :] = edge[h3:]

    outs = []

    def write(src, dst):
        copy = pltpu.make_async_copy(src, dst, out_sem.at[len(outs)])
        copy.start()
        outs.append(copy)

    used = 3 * ba * br
    lane = lax.broadcasted_iota(jnp.int32, (ch_rows, lanes), 1)

    def soften(i, carry):
        at = pl.multiple_of(i * ch_rows, ch_rows)
        f = feats[pl.ds(at, ch_rows), :]
        logits = lax.dot_general(
            f, wdp[...], (((1,), (1,)), ((), ())), preferred_element_type=jnp.float32
        )
        e = jnp.exp(-jnp.abs(logits))
        soft = jnp.maximum(logits, 0.0) + jnp.log1p(e) + 0.05
        soft = jnp.where(lane < bins_n, soft, 0.0)
        inv = 1.0 / jnp.sum(soft, axis=1, keepdims=True)
        p = soft * inv
        probs[pl.ds(at, ch_rows), :] = p
        slope[pl.ds(at, ch_rows), :] = logits
        sums[pl.ds(at, ch_rows), :] = inv
        low[pl.ds(at, ch_rows), :] = p.astype(jnp.bfloat16)
        return carry

    lax.fori_loop(0, cols // CH, soften, 0)

    def lift(i, carry):
        for c in range(CH):
            j = i * CH + c
            at = pl.multiple_of(j * height, height)
            a = lax.dot_general(
                low[pl.ds(at, height), :],
                pick_of(row_id, codes, j),
                (((1,), (1,)), ((), ())),
                preferred_element_type=jnp.float32,
            )
            amat[pl.ds(at, height), :] = a.astype(jnp.bfloat16)
        return carry

    lax.fori_loop(0, cols // CH, lift, 0)

    def gather(i, carry):
        at = pl.multiple_of(i * 2 * ch_rows, 2 * ch_rows)
        parts[...] += lax.dot_general(
            amat[pl.ds(at, 2 * ch_rows), :],
            feats[pl.ds(at, 2 * ch_rows), :],
            (((0,), (0,)), ((), ())),
            preferred_element_type=jnp.float32,
        )
        return carry

    lax.fori_loop(0, cols // (2 * CH), gather, 0)

    mine = parts[0:used, :]
    sendbuf[...] = mine.astype(jnp.bfloat16)
    n1, n2, n3 = (2 * ba + 2) * br, (ba + 2) * br, 2 * br
    send(sendbuf.at[pl.ds(used - n1, n1)], rp1, 1)
    send(sendbuf.at[pl.ds(0, n1)], rm1, -1)
    send(sendbuf.at[pl.ds(used - n2, n2)], rp2, 2)
    send(sendbuf.at[pl.ds(0, n2)], rm2, -2)
    send(sendbuf.at[pl.ds(used - n3, n3)], rp3, 3)
    send(sendbuf.at[pl.ds(0, n3)], rm3, -3)
    write(feats, feats_o)
    write(amat, amat_o)
    write(probs, probs_o)

    def bend(i, carry):
        at = pl.multiple_of(i * ch_rows, ch_rows)
        sig = jax.nn.sigmoid(slope[pl.ds(at, ch_rows), :]) * sums[pl.ds(at, ch_rows), :]
        slope[pl.ds(at, ch_rows), :] = jnp.where(lane < bins_n, sig, 0.0)
        return carry

    lax.fori_loop(0, cols // CH, bend, 0)
    for copy in messages[2:10]:
        copy.wait_recv()
    fetches[layers].wait()
    channels = feats.shape[1]
    total = win.shape[0]
    act_rows = total - 2 * br

    def merge(source, lo, hi):
        x = jnp.concatenate([source[i * br : i * br + act_rows] for i in range(3)], axis=1)
        z = [
            jnp.dot(
                x,
                mw[3 * dy : 3 * dy + 3, lo:hi, :].reshape(3 * (hi - lo), -1),
                preferred_element_type=jnp.float32,
            )
            for dy in range(3)
        ]
        return rolled_sum(z[0], z[1], z[2], br)

    lid_act = merge(lidwin[...], channels, mw.shape[1])
    write(slope, slope_o)
    win[...] = jnp.zeros_like(win)
    win[pl.ds(2 * br, used), :] = mine
    for copy in messages[10:]:
        copy.wait_recv()
    for got, size in ((rp1, n1), (rp2, n2), (rp3, n3)):
        win[pl.ds(0, size), :] += got[...].astype(jnp.float32)
    for got, size in ((rm1, n1), (rm2, n2), (rm3, n3)):
        win[pl.ds(total - size, size), :] += got[...].astype(jnp.float32)

    act = lid_act + merge(win[...].astype(jnp.bfloat16), 0, channels)
    gate = 1.0 / (1.0 + jnp.exp(-act))
    merged = (act * gate)[cot_own : cot_own + sec]
    merged_o[...] = jnp.stack(
        [merged[a * br : (a + 1) * br] for a in range(ba)], axis=1
    ).astype(jnp.bfloat16)
    grad_pre = (
        cotwin[...].astype(jnp.float32) * (gate * (1.0 + act * (1.0 - gate)))
    ).astype(jnp.bfloat16)

    def merge_back(first, rows, lo, hi):
        y = []
        for dy in range(3):
            acc = None
            for i in range(3):
                term = lax.dot_general(
                    grad_pre[first + (2 - i) * br : first + (2 - i) * br + rows],
                    mw[3 * dy + i, lo:hi, :],
                    (((1,), (1,)), ((), ())),
                    preferred_element_type=jnp.float32,
                )
                acc = term if acc is None else acc + term
            y.append(acc)
        return rolled_sum(y[2], y[1], y[0], br)

    table[...] = merge_back(0, used, 0, channels).astype(jnp.bfloat16)
    lid_grad = merge_back(sec, sec, channels, mw.shape[1])
    lidgrad_o[...] = jnp.stack(
        [lid_grad[a * br : (a + 1) * br] for a in range(ba)], axis=1
    ).astype(jnp.bfloat16)
    for copy in messages:
        copy.wait_send()
    for copy in outs:
        copy.wait()


def back_kernel(
    height, bins_n,
    feats, amat, probs, slope, codes, table, wd, merged, lid_grad,
    camgrad_o, merged_o, lidgrad_o,
    wdp, row_id,
):
    step = pl.program_id(0)
    ch_rows = CH * height

    @pl.when(step == 0)
    def _():
        merged_o[...] = merged[...]
        lidgrad_o[...] = lid_grad[...]
        wdp[...] = jnp.zeros_like(wdp)
        wdp[0:bins_n, :] = wd[...]
        row_id[...] = row_numbers(row_id.shape)

    turn = block_turn()
    blocks = []
    chunks = feats.shape[0] // ch_rows
    tab = table[...]
    for k in range(chunks):
        rows = pl.ds(k * ch_rows, ch_rows)
        g = lax.dot_general(
            feats[rows, :], tab, (((1,), (1,)), ((), ())), preferred_element_type=jnp.float32
        ).astype(jnp.bfloat16)
        direct = jnp.dot(amat[rows, :], tab, preferred_element_type=jnp.float32)
        gp = jnp.concatenate(
            [
                jnp.dot(
                    g[c * height : (c + 1) * height],
                    pick_of(row_id, codes, (step * chunks + k) * CH + c),
                    preferred_element_type=jnp.float32,
                )
                for c in range(CH)
            ],
            axis=0,
        )
        mean = jnp.sum(gp * probs[rows, :], axis=1, keepdims=True)
        gl = ((gp - mean) * slope[rows, :]).astype(jnp.bfloat16)
        depth = jnp.dot(gl, wdp[...], preferred_element_type=jnp.float32)
        blocks.append((direct + depth).astype(jnp.bfloat16))
    block = jnp.concatenate(blocks, axis=0)
    for h0 in range(0, height, BLOCK):
        part = jnp.concatenate(
            [block[c * height + h0 : c * height + h0 + BLOCK] for c in range(BLOCK)], axis=0
        )
        turned = jnp.dot(turn, part, preferred_element_type=jnp.float32)
        camgrad_o[h0 : h0 + BLOCK, :, :] = turned.astype(jnp.bfloat16).reshape(
            BLOCK, BLOCK, -1
        )


def local(
    n, strips,
    image_feats, cam_weights, depth_weight, ray_bins, pillar_sums, pillar_counts,
    lidar_weight, merge_weight, out_cotangent,
):
    height, cols, channels = image_feats.shape
    br, ba, cf = out_cotangent.shape
    bins_n = depth_weight.shape[1]
    cl = pillar_sums.shape[2]
    lanes = -(-bins_n // 128) * 128
    used = groups = 3 * ba * br
    total = (3 * ba + 4) * br
    bf, f32 = jnp.bfloat16, jnp.float32

    vm = pl.BlockSpec(memory_space=pltpu.VMEM)
    hbm = pl.BlockSpec(memory_space=pl.ANY)
    n1, n2, n3 = (2 * ba + 2) * br, (ba + 2) * br, 2 * br
    rows = cols * height
    merged, lid_grad, table, codes, feats, amat, probs, slope = pl.pallas_call(
        functools.partial(kernel, n, strips, cols, height, br, ba, bins_n),
        out_shape=(
            jax.ShapeDtypeStruct((br, ba, cf), bf),
            jax.ShapeDtypeStruct((br, ba, cl), bf),
            jax.ShapeDtypeStruct((groups, channels), bf),
            jax.ShapeDtypeStruct((cols, lanes), f32),
            jax.ShapeDtypeStruct((rows, channels), bf),
            jax.ShapeDtypeStruct((rows, groups), bf),
            jax.ShapeDtypeStruct((rows, lanes), f32),
            jax.ShapeDtypeStruct((rows, lanes), f32),
        ),
        in_specs=[hbm, hbm, vm, vm, vm, vm, vm, vm, hbm],
        out_specs=(vm,) * 4 + (hbm,) * 4,
        scratch_shapes=[
            pltpu.VMEM(image_feats.shape, bf),
            pltpu.VMEM(cam_weights.shape, bf),
            pltpu.VMEM(merge_weight.shape, bf),
            pltpu.VMEM(((cols + 6) * height, channels), bf),
            pltpu.VMEM(((cols + 4) * height, channels), bf),
            pltpu.VMEM(((cols + 2) * height, channels), bf),
            pltpu.VMEM((cols * height, channels), bf),
            pltpu.VMEM((lanes, channels), bf),
            pltpu.VMEM((cols * height, lanes), f32),
            pltpu.VMEM((cols * height, lanes), f32),
            pltpu.VMEM((cols * height, 1), f32),
            pltpu.VMEM((cols * height, lanes), bf),
            pltpu.VMEM((groups, lanes), bf),
            pltpu.VMEM((cols * height, groups), bf),
            pltpu.VMEM((groups, channels), f32),
            pltpu.VMEM((used, channels), bf),
            pltpu.VMEM((n1, channels), bf),
            pltpu.VMEM((n2, channels), bf),
            pltpu.VMEM((n3, channels), bf),
            pltpu.VMEM((n1, channels), bf),
            pltpu.VMEM((n2, channels), bf),
            pltpu.VMEM((n3, channels), bf),
            pltpu.VMEM((total, channels), f32),
            pltpu.VMEM((total, cl), bf),
            pltpu.VMEM((total - 2 * br, cf), bf),
            pltpu.SemaphoreType.DMA((cam_weights.shape[0] + 2,)),
            pltpu.SemaphoreType.DMA((4,)),
            pltpu.SemaphoreType.DMA((16,)),
            pltpu.SemaphoreType.DMA((16,)),
        ],
        compiler_params=pltpu.CompilerParams(
            collective_id=0, has_side_effects=True, vmem_limit_bytes=58 * 1024 * 1024
        ),
        name="bev",
    )(
        image_feats, cam_weights, depth_weight.T, ray_bins, pillar_sums, pillar_counts.T,
        lidar_weight, out_cotangent, merge_weight,
    )
    steps = cols // BLOCK

    def rowed(width):
        return pl.BlockSpec((rows // steps, width), lambda i: (i, 0))

    def whole(*shape):
        return pl.BlockSpec(shape, lambda i: (0,) * len(shape))

    cam_grad, merged, lid_grad = pl.pallas_call(
        functools.partial(back_kernel, height, bins_n),
        grid=(steps,),
        out_shape=(
            jax.ShapeDtypeStruct((height, cols, channels), bf),
            jax.ShapeDtypeStruct((br, ba, cf), bf),
            jax.ShapeDtypeStruct((br, ba, cl), bf),
        ),
        in_specs=[
            rowed(channels), rowed(groups), rowed(lanes), rowed(lanes),
            whole(cols, lanes), whole(groups, channels), whole(bins_n, channels),
            whole(br, ba, cf), whole(br, ba, cl),
        ],
        out_specs=(
            pl.BlockSpec((height, cols // steps, channels), lambda i: (0, i, 0)),
            whole(br, ba, cf),
            whole(br, ba, cl),
        ),
        scratch_shapes=[pltpu.VMEM((lanes, channels), bf), pltpu.VMEM((groups, lanes), bf)],
        name="back",
    )(feats, amat, probs, slope, codes, table, depth_weight.T, merged, lid_grad)
    return merged, cam_grad, lid_grad


def solution(mesh):
    strips = mesh.shape["strip"]
    n = mesh.shape["branch"] * strips
    placed = (
        P(None, AXES, None),
        P(),
        P(),
        P(AXES, None),
        P(None, AXES, None),
        P(None, AXES),
        P(),
        P(),
        P(None, AXES, None),
    )
    return jax.shard_map(
        functools.partial(local, n, strips),
        mesh=mesh,
        in_specs=placed,
        out_specs=(P(None, AXES, None),) * 3,
        check_vma=False,
    )
```

profile of v0, /device:TPU:0, one launch (start us, length us, event | category | flops | bytes accessed | tf_op | source)
XLA Modules:
  0.0 39.8 jit_solution(12511554124503083931)
XLA Ops:
  0.6 31.5 %bev.1 = (bf16[16,4,256]{2,1,0:T(4,128)(2,1)}, bf16[16,4,128]{2,1,0:T(4,128)(2,1)}, bf16[192,256]{1,0:T(8,128)(2,1)}, f32[64,128]{1,0:T(8,128)}, bf16[2048,256]{...) custom-call(bf16[32,64,256]{2,1,0:T(8,128)(2,1)} %img_hbm.1, ...), custom_call_target="tpu_custom_call" | custom-call | tf_op jit(solution)/shard_map/bev/pallas_call | solution.py:421
  32.2 7.6 %back.1 = (bf16[32,64,256]{2,1,0:T(8,128)(2,1)}, bf16[16,4,256]{2,1,0:T(4,128)(2,1)}, bf16[16,4,128]{2,1,0:T(4,128)(2,1)}) custom-call(bf16[2048,256]{1,0:T(8,128)(2,1)} %get-tuple-element.14.feats, bf16[2048,192]{1,0:T(8,128)(2,1)} %get-tuple-element.15.amat, f32[2048,128]{1,0:T(8,128)} %get-tuple-element.16.probs, f32[2048,128]{1,0:T(8,128)} %get-tuple-element.17.slope, ...), custom_call_target="tpu_custom_call" | custom-call | tf_op jit(solution)/shard_map/back/pallas_call | solution.py:482
where the time goes:
time: 40 us; the launch traced here: 39.8 us
  Pallas kernels  39.2 us (98%)
  between operations  0.64 us (2%)
    pallas_call x1, Pallas kernels, local(): pl.pallas_call(functools.partial(kernel, n, strips, cols, height, br, ba,...  31.5 us
    pallas_call x1, Pallas kernels, local(): pl.pallas_call(functools.partial(back_kernel, height, bins_n), grid=(step...  7.64 us

commit v1 on v0

--- a/solution.py
+++ b/solution.py
@@ -68,11 +68,12 @@
 
 def kernel(
     n, strips, cols, height, br, ba, bins_n,
-    img_hbm, cw_hbm, wd, bins, pillars, counts, lw, cot, mw_hbm,
-    merged_o, lidgrad_o, table, codes, feats_o, amat_o, probs_o, slope_o,
-    img, cw, mw, xin, y1, y2, feats, wdp, probs, slope, sums, low, row_id, amat, parts, sendbuf,
+    img_hbm, cw_hbm, wd_hbm, bins_hbm, pillars_hbm, counts_hbm, lw_hbm, cot_hbm, mw_hbm,
+    merged_o, lidgrad_o, table, codes, feats, amat, probs, slope,
+    img, cw, mw, xin, y1, y2, wd, bins, pillars, counts, lw, cot,
+    wdp, sums, low, row_id, parts, sendbuf,
     rp1, rp2, rp3, rm1, rm2, rm3, win, lidwin, cotwin,
-    local_sem, out_sem, send_sem, recv_sem,
+    local_sem, send_sem, recv_sem,
 ):
     me = lax.axis_index(AXES[0]) * strips + lax.axis_index(AXES[1])
     ch_rows = CH * height
@@ -88,6 +89,17 @@
             barrier, inc=1, device_id=dev(d), device_id_type=pl.DeviceIdType.MESH
         )
     layers = cw.shape[0]
+    small = [
+        pltpu.make_async_copy(src, dst, local_sem.at[layers + 2 + i])
+        for i, (src, dst) in enumerate(
+            (
+                (pillars_hbm, pillars), (counts_hbm, counts), (lw_hbm, lw), (cot_hbm, cot),
+                (wd_hbm, wd), (bins_hbm, bins),
+            )
+        )
+    ]
+    for copy in small:
+        copy.start()
     image = pltpu.make_async_copy(img_hbm, img, local_sem.at[layers + 1])
     image.start()
     fetches = [
@@ -97,6 +109,13 @@
     for copy in fetches:
         copy.start()
 
+    row_id[...] = row_numbers(row_id.shape)
+    wdp[...] = jnp.zeros_like(wdp)
+    codes[...] = jnp.full(codes.shape, -1.0, jnp.float32)
+    parts[...] = jnp.zeros_like(parts)
+    win[...] = jnp.zeros_like(win)
+    for copy in small:
+        copy.wait()
     sec = ba * br
     cot_own, lid_own = (ba + 1) * br, (ba + 2) * br
     cot_f = cot[...].astype(jnp.float32)
@@ -131,12 +150,8 @@
     off = jnp.where(off >= n, off - n, off)
     in_cell = raw & (cell - 1)
     code = (((off << sh_ba) + (in_cell & (ba - 1))) << sh_br) + (in_cell >> sh_ba)
-    codes[...] = jnp.full(codes.shape, -1.0, jnp.float32)
     codes[:, 0:bins_n] = code.astype(jnp.float32)
-    row_id[...] = row_numbers(row_id.shape)
-    wdp[...] = jnp.zeros_like(wdp)
     wdp[0:bins_n, :] = wd[...]
-    parts[...] = jnp.zeros_like(parts)
     image.wait()
     turn = block_turn()
     for j0 in range(0, cols, BLOCK):
@@ -205,13 +220,6 @@
         dst[pl.ds(0, h3), :] = edge[:h3]
         dst[pl.ds(right, size), :] = edge[h3:]
 
-    outs = []
-
-    def write(src, dst):
-        copy = pltpu.make_async_copy(src, dst, out_sem.at[len(outs)])
-        copy.start()
-        outs.append(copy)
-
     used = 3 * ba * br
     lane = lax.broadcasted_iota(jnp.int32, (ch_rows, lanes), 1)
 
@@ -270,9 +278,6 @@
     send(sendbuf.at[pl.ds(0, n2)], rm2, -2)
     send(sendbuf.at[pl.ds(used - n3, n3)], rp3, 3)
     send(sendbuf.at[pl.ds(0, n3)], rm3, -3)
-    write(feats, feats_o)
-    write(amat, amat_o)
-    write(probs, probs_o)
 
     def bend(i, carry):
         at = pl.multiple_of(i * ch_rows, ch_rows)
@@ -301,8 +306,6 @@
         return rolled_sum(z[0], z[1], z[2], br)
 
     lid_act = merge(lidwin[...], channels, mw.shape[1])
-    write(slope, slope_o)
-    win[...] = jnp.zeros_like(win)
     win[pl.ds(2 * br, used), :] = mine
     for copy in messages[10:]:
         copy.wait_recv()
@@ -343,61 +346,82 @@
     ).astype(jnp.bfloat16)
     for copy in messages:
         copy.wait_send()
-    for copy in outs:
-        copy.wait()
 
 
 def back_kernel(
-    height, bins_n,
+    height, bins_n, steps,
     feats, amat, probs, slope, codes, table, wd, merged, lid_grad,
     camgrad_o, merged_o, lidgrad_o,
-    wdp, row_id,
+    wdp, row_id, buf, sem,
 ):
-    step = pl.program_id(0)
     ch_rows = CH * height
-
-    @pl.when(step == 0)
-    def _():
-        merged_o[...] = merged[...]
-        lidgrad_o[...] = lid_grad[...]
-        wdp[...] = jnp.zeros_like(wdp)
-        wdp[0:bins_n, :] = wd[...]
-        row_id[...] = row_numbers(row_id.shape)
-
+    small = [
+        pltpu.make_async_copy(merged, merged_o, sem.at[2]),
+        pltpu.make_async_copy(lid_grad, lidgrad_o, sem.at[3]),
+    ]
+    for copy in small:
+        copy.start()
+    wdp[...] = jnp.zeros_like(wdp)
+    wdp[0:bins_n, :] = wd[...]
+    row_id[...] = row_numbers(row_id.shape)
     turn = block_turn()
-    blocks = []
-    chunks = feats.shape[0] // ch_rows
-    tab = table[...]
-    for k in range(chunks):
-        rows = pl.ds(k * ch_rows, ch_rows)
-        g = lax.dot_general(
-            feats[rows, :], tab, (((1,), (1,)), ((), ())), preferred_element_type=jnp.float32
-        ).astype(jnp.bfloat16)
-        direct = jnp.dot(amat[rows, :], tab, preferred_element_type=jnp.float32)
-        gp = jnp.concatenate(
-            [
-                jnp.dot(
-                    g[c * height : (c + 1) * height],
-                    pick_of(row_id, codes, (step * chunks + k) * CH + c),
-                    preferred_element_type=jnp.float32,
-                )
-                for c in range(CH)
-            ],
-            axis=0,
-        )
-        mean = jnp.sum(gp * probs[rows, :], axis=1, keepdims=True)
-        gl = ((gp - mean) * slope[rows, :]).astype(jnp.bfloat16)
-        depth = jnp.dot(gl, wdp[...], preferred_element_type=jnp.float32)
-        blocks.append((direct + depth).astype(jnp.bfloat16))
-    block = jnp.concatenate(blocks, axis=0)
-    for h0 in range(0, height, BLOCK):
-        part = jnp.concatenate(
-            [block[c * height + h0 : c * height + h0 + BLOCK] for c in range(BLOCK)], axis=0
-        )
-        turned = jnp.dot(turn, part, preferred_element_type=jnp.float32)
-        camgrad_o[h0 : h0 + BLOCK, :, :] = turned.astype(jnp.bfloat16).reshape(
-            BLOCK, BLOCK, -1
-        )
+    chunks = BLOCK // CH
+
+    def out_copy(step, slot):
+        return pltpu.make_async_copy(
+            buf.at[slot],
+            camgrad_o.at[:, pl.ds(pl.multiple_of(step * BLOCK, BLOCK), BLOCK), :],
+            sem.at[slot],
+        )
+
+    def body(step, carry):
+        slot = step & 1
+
+        @pl.when(step >= 2)
+        def _():
+            out_copy(step - 2, slot).wait()
+
+        tab = table[...]
+        blocks = []
+        for k in range(chunks):
+            at = pl.multiple_of((step * chunks + k) * ch_rows, ch_rows)
+            rows = pl.ds(at, ch_rows)
+            g = lax.dot_general(
+                feats[rows, :], tab, (((1,), (1,)), ((), ())), preferred_element_type=jnp.float32
+            ).astype(jnp.bfloat16)
+            direct = jnp.dot(amat[rows, :], tab, preferred_element_type=jnp.float32)
+            gp = jnp.concatenate(
+                [
+                    jnp.dot(
+                        g[c * height : (c + 1) * height],
+                        pick_of(row_id, codes, (step * chunks + k) * CH + c),
+                        preferred_element_type=jnp.float32,
+                    )
+                    for c in range(CH)
+                ],
+                axis=0,
+            )
+            mean = jnp.sum(gp * probs[rows, :], axis=1, keepdims=True)
+            gl = ((gp - mean) * slope[rows, :]).astype(jnp.bfloat16)
+            depth = jnp.dot(gl, wdp[...], preferred_element_type=jnp.float32)
+            blocks.append((direct + depth).astype(jnp.bfloat16))
+        block = jnp.concatenate(blocks, axis=0)
+        for h0 in range(0, height, BLOCK):
+            part = jnp.concatenate(
+                [block[c * height + h0 : c * height + h0 + BLOCK] for c in range(BLOCK)], axis=0
+            )
+            turned = jnp.dot(turn, part, preferred_element_type=jnp.float32)
+            buf[slot, h0 : h0 + BLOCK, :, :] = turned.astype(jnp.bfloat16).reshape(
+                BLOCK, BLOCK, -1
+            )
+        out_copy(step, slot).start()
+        return carry
+
+    lax.fori_loop(0, steps, body, 0)
+    for k in (2, 1):
+        out_copy(steps - k, (steps - k) & 1).wait()
+    for copy in small:
+        copy.wait()
 
 
 def local(
@@ -415,23 +439,25 @@
     bf, f32 = jnp.bfloat16, jnp.float32
 
     vm = pl.BlockSpec(memory_space=pltpu.VMEM)
-    hbm = pl.BlockSpec(memory_space=pl.ANY)
+    hbm = pl.BlockSpec(memory_space=pltpu.HBM)
     n1, n2, n3 = (2 * ba + 2) * br, (ba + 2) * br, 2 * br
     rows = cols * height
+    turned_counts = pillar_counts.T
+    turned_depth = depth_weight.T
     merged, lid_grad, table, codes, feats, amat, probs, slope = pl.pallas_call(
         functools.partial(kernel, n, strips, cols, height, br, ba, bins_n),
         out_shape=(
-            jax.ShapeDtypeStruct((br, ba, cf), bf),
-            jax.ShapeDtypeStruct((br, ba, cl), bf),
-            jax.ShapeDtypeStruct((groups, channels), bf),
-            jax.ShapeDtypeStruct((cols, lanes), f32),
-            jax.ShapeDtypeStruct((rows, channels), bf),
-            jax.ShapeDtypeStruct((rows, groups), bf),
-            jax.ShapeDtypeStruct((rows, lanes), f32),
-            jax.ShapeDtypeStruct((rows, lanes), f32),
+            pltpu.VMEM((br, ba, cf), bf),
+            pltpu.VMEM((br, ba, cl), bf),
+            pltpu.VMEM((groups, channels), bf),
+            pltpu.VMEM((cols, lanes), f32),
+            pltpu.VMEM((rows, channels), bf),
+            pltpu.VMEM((rows, groups), bf),
+            pltpu.VMEM((rows, lanes), f32),
+            pltpu.VMEM((rows, lanes), f32),
         ),
-        in_specs=[hbm, hbm, vm, vm, vm, vm, vm, vm, hbm],
-        out_specs=(vm,) * 4 + (hbm,) * 4,
+        in_specs=[hbm] * 9,
+        out_specs=(vm,) * 8,
         scratch_shapes=[
             pltpu.VMEM(image_feats.shape, bf),
             pltpu.VMEM(cam_weights.shape, bf),
@@ -439,14 +465,16 @@
             pltpu.VMEM(((cols + 6) * height, channels), bf),
             pltpu.VMEM(((cols + 4) * height, channels), bf),
             pltpu.VMEM(((cols + 2) * height, channels), bf),
-            pltpu.VMEM((cols * height, channels), bf),
+            pltpu.VMEM(turned_depth.shape, bf),
+            pltpu.VMEM(ray_bins.shape, jnp.int32),
+            pltpu.VMEM(pillar_sums.shape, bf),
+            pltpu.VMEM(turned_counts.shape, jnp.int32),
+            pltpu.VMEM(lidar_weight.shape, bf),
+            pltpu.VMEM(out_cotangent.shape, bf),
             pltpu.VMEM((lanes, channels), bf),
-            pltpu.VMEM((cols * height, lanes), f32),
-            pltpu.VMEM((cols * height, lanes), f32),
             pltpu.VMEM((cols * height, 1), f32),
             pltpu.VMEM((cols * height, lanes), bf),
             pltpu.VMEM((groups, lanes), bf),
-            pltpu.VMEM((cols * height, groups), bf),
             pltpu.VMEM((groups, channels), f32),
             pltpu.VMEM((used, channels), bf),
             pltpu.VMEM((n1, channels), bf),
@@ -458,48 +486,42 @@
             pltpu.VMEM((total, channels), f32),
             pltpu.VMEM((total, cl), bf),
             pltpu.VMEM((total - 2 * br, cf), bf),
-            pltpu.SemaphoreType.DMA((cam_weights.shape[0] + 2,)),
-            pltpu.SemaphoreType.DMA((4,)),
+            pltpu.SemaphoreType.DMA((cam_weights.shape[0] + 8,)),
             pltpu.SemaphoreType.DMA((16,)),
             pltpu.SemaphoreType.DMA((16,)),
         ],
         compiler_params=pltpu.CompilerParams(
-            collective_id=0, has_side_effects=True, vmem_limit_bytes=58 * 1024 * 1024
+            collective_id=0, has_side_effects=True, vmem_limit_bytes=40 * 1024 * 1024
         ),
         name="bev",
     )(
-        image_feats, cam_weights, depth_weight.T, ray_bins, pillar_sums, pillar_counts.T,
-        lidar_weight, out_cotangent, merge_weight,
+        *(
+            pltpu.with_memory_space_constraint(x, pltpu.HBM)
+            for x in (
+                image_feats, cam_weights, turned_depth, ray_bins, pillar_sums, turned_counts,
+                lidar_weight, out_cotangent, merge_weight,
+            )
+        )
     )
     steps = cols // BLOCK
-
-    def rowed(width):
-        return pl.BlockSpec((rows // steps, width), lambda i: (i, 0))
-
-    def whole(*shape):
-        return pl.BlockSpec(shape, lambda i: (0,) * len(shape))
-
     cam_grad, merged, lid_grad = pl.pallas_call(
-        functools.partial(back_kernel, height, bins_n),
-        grid=(steps,),
+        functools.partial(back_kernel, height, bins_n, steps),
         out_shape=(
-            jax.ShapeDtypeStruct((height, cols, channels), bf),
-            jax.ShapeDtypeStruct((br, ba, cf), bf),
-            jax.ShapeDtypeStruct((br, ba, cl), bf),
+            pltpu.HBM((height, cols, channels), bf),
+            pltpu.HBM((br, ba, cf), bf),
+            pltpu.HBM((br, ba, cl), bf),
         ),
-        in_specs=[
-            rowed(channels), rowed(groups), rowed(lanes), rowed(lanes),
-            whole(cols, lanes), whole(groups, channels), whole(bins_n, channels),
-            whole(br, ba, cf), whole(br, ba, cl),
+        in_specs=[vm] * 9,
+        out_specs=(hbm,) * 3,
+        scratch_shapes=[
+            pltpu.VMEM((lanes, channels), bf),
+            pltpu.VMEM((groups, lanes), bf),
+            pltpu.VMEM((2, height, BLOCK, channels), bf),
+            pltpu.SemaphoreType.DMA((4,)),
         ],
-        out_specs=(
-            pl.BlockSpec((height, cols // steps, channels), lambda i: (0, i, 0)),
-            whole(br, ba, cf),
-            whole(br, ba, cl),
-        ),
-        scratch_shapes=[pltpu.VMEM((lanes, channels), bf), pltpu.VMEM((groups, lanes), bf)],
+        compiler_params=pltpu.CompilerParams(vmem_limit_bytes=40 * 1024 * 1024),
         name="back",
-    )(feats, amat, probs, slope, codes, table, depth_weight.T, merged, lid_grad)
+    )(feats, amat, probs, slope, codes, table, turned_depth, merged, lid_grad)
     return merged, cam_grad, lid_grad
 
 

time: 40 us -> 37.3 us (0.932)
  Pallas kernels: 39.2 us -> 36.5 us
    pallas_call x1, Pallas kernels: 7.64 us -> 6.24 us  [local(): pl.pallas_call(functools.partial(back_kernel, height, bins_n, steps), out...]
    pallas_call x1, Pallas kernels: 31.5 us -> 30.3 us  [local(): pl.pallas_call(functools.partial(kernel, n, strips, cols, height, br, ba,...]
where the time goes in v1:
time: 37.3 us; the launch traced here: 37.2 us
  Pallas kernels  36.5 us (98%)
  between operations  0.66 us (2%)
    pallas_call x1, Pallas kernels, local(): pl.pallas_call(functools.partial(kernel, n, strips, cols, height, br, ba,...  30.3 us
    pallas_call x1, Pallas kernels, local(): pl.pallas_call(functools.partial(back_kernel, height, bins_n, steps), out...  6.24 us

profile of v1, /device:TPU:0, one launch (start us, length us, event | category | flops | bytes accessed | tf_op | source)
XLA Modules:
  0.0 37.2 jit_solution(12345116303683387042)
XLA Ops:
  0.6 0.0 copy-start
  0.6 30.3 %bev.1 = (bf16[16,4,256]{2,1,0:T(4,128)(2,1)S(1)}, bf16[16,4,128]{2,1,0:T(4,128)(2,1)S(1)}, bf16[192,256]{1,0:T(8,128)(2,1)S(1)}, f32[64,128]{1,0:T(8,128)S(1)},...) custom-call(bf16[32,64,256]{2,1,0:T(8,128)(2,1)} %img_hbm.1, ...), custom_call_target="tpu_custom_call" | custom-call | tf_op jit(solution)/shard_map/bev/pallas_call | solution.py:447
  30.9 0.0 copy-done
  30.9 6.2 %back.1 = (bf16[32,64,256]{2,1,0:T(8,128)(2,1)}, bf16[16,4,256]{2,1,0:T(4,128)(2,1)}, bf16[16,4,128]{2,1,0:T(4,128)(2,1)}) custom-call(bf16[2048,256]{1,0:T(8,128)(2,1)S(1)} %get-tuple-element.14.feats, bf16[2048,192]{1,0:T(8,128)(2,1)S(1)} %get-tuple-element.15.amat, f32[2048,128]{1,0:T(8,128)S(1)} %get-tuple-element.16.probs, ...), custom_call_target="tpu_custom_call" | custom-call | tf_op jit(solution)/shard_map/back/pallas_call | solution.py:507
Async XLA Ops:
  0.6 30.3 %copy-start = (bf16[256,118]{0,1:T(8,128)(2,1)S(1)}, bf16[256,118]{0,1:T(8,128)(2,1)}, u32[]{:S(2)}) copy-start(bf16[256,118]{0,1:T(8,128)(2,1)} %param.11) | copy-start | bytes 181252

commit v2 on v1

--- a/solution.py
+++ b/solution.py
@@ -49,12 +49,15 @@
     return lax.broadcasted_iota(jnp.int32, shape, 0).astype(jnp.float32).astype(jnp.bfloat16)
 
 
+def one_hot(hit):
+    return jnp.where(hit, jnp.ones((), jnp.bfloat16), jnp.zeros((), jnp.bfloat16))
+
+
 def pick_of(row_id, codes, j):
     groups, lanes = row_id.shape
     code = jnp.broadcast_to(codes[pl.ds(j, 1), :], (16, lanes)).astype(jnp.bfloat16)
     code = jnp.concatenate([code] * (groups // 16), axis=0)
-    one, zero = jnp.ones((), jnp.bfloat16), jnp.zeros((), jnp.bfloat16)
-    return jnp.where(row_id[...] == code, one, zero)
+    return one_hot(row_id[...] == code)
 
 
 def block_turn():
@@ -69,9 +72,9 @@
 def kernel(
     n, strips, cols, height, br, ba, bins_n,
     img_hbm, cw_hbm, wd_hbm, bins_hbm, pillars_hbm, counts_hbm, lw_hbm, cot_hbm, mw_hbm,
-    merged_o, lidgrad_o, table, codes, feats, amat, probs, slope,
+    merged_o, lidgrad_o, table, picks, feats, amat, probs, slope,
     img, cw, mw, xin, y1, y2, wd, bins, pillars, counts, lw, cot,
-    wdp, sums, low, row_id, parts, sendbuf,
+    wdp, sums, low, row_id, codes, routes, sendbuf,
     rp1, rp2, rp3, rm1, rm2, rm3, win, lidwin, cotwin,
     local_sem, send_sem, recv_sem,
 ):
@@ -93,8 +96,8 @@
         pltpu.make_async_copy(src, dst, local_sem.at[layers + 2 + i])
         for i, (src, dst) in enumerate(
             (
-                (pillars_hbm, pillars), (counts_hbm, counts), (lw_hbm, lw), (cot_hbm, cot),
-                (wd_hbm, wd), (bins_hbm, bins),
+                (bins_hbm, bins), (pillars_hbm, pillars), (counts_hbm, counts), (lw_hbm, lw),
+                (cot_hbm, cot), (wd_hbm, wd),
             )
         )
     ]
@@ -112,9 +115,24 @@
     row_id[...] = row_numbers(row_id.shape)
     wdp[...] = jnp.zeros_like(wdp)
     codes[...] = jnp.full(codes.shape, -1.0, jnp.float32)
-    parts[...] = jnp.zeros_like(parts)
     win[...] = jnp.zeros_like(win)
-    for copy in small:
+    small[0].wait()
+    cell = br * ba
+    sh_cell, sh_ba, sh_br = cell.bit_length() - 1, ba.bit_length() - 1, br.bit_length() - 1
+    raw = bins[...]
+    off = (raw >> sh_cell) - me + 1
+    off = jnp.where(off < 0, off + n, off)
+    off = jnp.where(off >= n, off - n, off)
+    in_cell = raw & (cell - 1)
+    code = (((off << sh_ba) + (in_cell & (ba - 1))) << sh_br) + (in_cell >> sh_ba)
+    codes[:, 0:bins_n] = code.astype(jnp.float32)
+    turned_codes = jnp.transpose(codes[...])
+    cells = lax.broadcasted_iota(jnp.int32, routes.shape[1:], 1)
+    cells = cells.astype(jnp.float32).astype(jnp.bfloat16)
+    for j in range(cols):
+        code = jnp.broadcast_to(turned_codes[:, j : j + 1], cells.shape).astype(jnp.bfloat16)
+        routes[j] = one_hot(code == cells)
+    for copy in small[1:]:
         copy.wait()
     sec = ba * br
     cot_own, lid_own = (ba + 1) * br, (ba + 2) * br
@@ -142,15 +160,6 @@
     )
     lidwin[pl.ds(lid_own, sec), :] = jnp.maximum(lid, 0.0).astype(jnp.bfloat16)
 
-    cell = br * ba
-    sh_cell, sh_ba, sh_br = cell.bit_length() - 1, ba.bit_length() - 1, br.bit_length() - 1
-    raw = bins[...]
-    off = (raw >> sh_cell) - me + 1
-    off = jnp.where(off < 0, off + n, off)
-    off = jnp.where(off >= n, off - n, off)
-    in_cell = raw & (cell - 1)
-    code = (((off << sh_ba) + (in_cell & (ba - 1))) << sh_br) + (in_cell >> sh_ba)
-    codes[:, 0:bins_n] = code.astype(jnp.float32)
     wdp[0:bins_n, :] = wd[...]
     image.wait()
     turn = block_turn()
@@ -221,55 +230,29 @@
         dst[pl.ds(right, size), :] = edge[h3:]
 
     used = 3 * ba * br
-    lane = lax.broadcasted_iota(jnp.int32, (ch_rows, lanes), 1)
-
-    def soften(i, carry):
-        at = pl.multiple_of(i * ch_rows, ch_rows)
-        f = feats[pl.ds(at, ch_rows), :]
+    wide = 2 * CH * height
+    lane = lax.broadcasted_iota(jnp.int32, (wide, lanes), 1)
+    for at in range(0, cols * height, wide):
+        rows = pl.ds(at, wide)
         logits = lax.dot_general(
-            f, wdp[...], (((1,), (1,)), ((), ())), preferred_element_type=jnp.float32
+            feats[rows, :], wdp[...], (((1,), (1,)), ((), ())), preferred_element_type=jnp.float32
         )
         e = jnp.exp(-jnp.abs(logits))
-        soft = jnp.maximum(logits, 0.0) + jnp.log1p(e) + 0.05
+        soft = jnp.maximum(logits, 0.0) + jnp.log(1.0 + e) + 0.05
         soft = jnp.where(lane < bins_n, soft, 0.0)
         inv = 1.0 / jnp.sum(soft, axis=1, keepdims=True)
         p = soft * inv
-        probs[pl.ds(at, ch_rows), :] = p
-        slope[pl.ds(at, ch_rows), :] = logits
-        sums[pl.ds(at, ch_rows), :] = inv
-        low[pl.ds(at, ch_rows), :] = p.astype(jnp.bfloat16)
-        return carry
-
-    lax.fori_loop(0, cols // CH, soften, 0)
-
-    def lift(i, carry):
-        for c in range(CH):
-            j = i * CH + c
-            at = pl.multiple_of(j * height, height)
-            a = lax.dot_general(
-                low[pl.ds(at, height), :],
-                pick_of(row_id, codes, j),
-                (((1,), (1,)), ((), ())),
-                preferred_element_type=jnp.float32,
-            )
-            amat[pl.ds(at, height), :] = a.astype(jnp.bfloat16)
-        return carry
-
-    lax.fori_loop(0, cols // CH, lift, 0)
-
-    def gather(i, carry):
-        at = pl.multiple_of(i * 2 * ch_rows, 2 * ch_rows)
-        parts[...] += lax.dot_general(
-            amat[pl.ds(at, 2 * ch_rows), :],
-            feats[pl.ds(at, 2 * ch_rows), :],
-            (((0,), (0,)), ((), ())),
-            preferred_element_type=jnp.float32,
-        )
-        return carry
-
-    lax.fori_loop(0, cols // (2 * CH), gather, 0)
-
-    mine = parts[0:used, :]
+        probs[rows, :] = p
+        slope[rows, :] = logits
+        sums[rows, :] = inv
+        low[rows, :] = p.astype(jnp.bfloat16)
+    for j in range(cols):
+        rows = pl.ds(j * height, height)
+        a = jnp.dot(low[rows, :], routes[j], preferred_element_type=jnp.float32)
+        amat[rows, :] = a.astype(jnp.bfloat16)
+    mine = lax.dot_general(
+        amat[...], feats[...], (((0,), (0,)), ((), ())), preferred_element_type=jnp.float32
+    )
     sendbuf[...] = mine.astype(jnp.bfloat16)
     n1, n2, n3 = (2 * ba + 2) * br, (ba + 2) * br, 2 * br
     send(sendbuf.at[pl.ds(used - n1, n1)], rp1, 1)
@@ -279,13 +262,14 @@
     send(sendbuf.at[pl.ds(used - n3, n3)], rp3, 3)
     send(sendbuf.at[pl.ds(0, n3)], rm3, -3)
 
-    def bend(i, carry):
-        at = pl.multiple_of(i * ch_rows, ch_rows)
-        sig = jax.nn.sigmoid(slope[pl.ds(at, ch_rows), :]) * sums[pl.ds(at, ch_rows), :]
-        slope[pl.ds(at, ch_rows), :] = jnp.where(lane < bins_n, sig, 0.0)
-        return carry
-
-    lax.fori_loop(0, cols // CH, bend, 0)
+    for at in range(0, cols * height, wide):
+        rows = pl.ds(at, wide)
+        sig = jax.nn.sigmoid(slope[rows, :]) * sums[rows, :]
+        slope[rows, :] = jnp.where(lane < bins_n, sig, 0.0)
+    for j in range(0, cols, 2):
+        picks[j // 2] = jnp.concatenate(
+            [pick_of(row_id, codes, j), pick_of(row_id, codes, j + 1)], axis=1
+        )
     for copy in messages[2:10]:
         copy.wait_recv()
     fetches[layers].wait()
@@ -350,77 +334,55 @@
 
 def back_kernel(
     height, bins_n, steps,
-    feats, amat, probs, slope, codes, table, wd, merged, lid_grad,
+    feats, amat, probs, slope, picks, table, wd, merged, lid_grad,
     camgrad_o, merged_o, lidgrad_o,
-    wdp, row_id, buf, sem,
+    wdp, buf, sem,
 ):
-    ch_rows = CH * height
-    small = [
-        pltpu.make_async_copy(merged, merged_o, sem.at[2]),
-        pltpu.make_async_copy(lid_grad, lidgrad_o, sem.at[3]),
+    lanes = wdp.shape[0]
+    copies = [
+        pltpu.make_async_copy(merged, merged_o, sem.at[steps]),
+        pltpu.make_async_copy(lid_grad, lidgrad_o, sem.at[steps + 1]),
     ]
-    for copy in small:
+    for copy in copies:
         copy.start()
     wdp[...] = jnp.zeros_like(wdp)
     wdp[0:bins_n, :] = wd[...]
-    row_id[...] = row_numbers(row_id.shape)
     turn = block_turn()
-    chunks = BLOCK // CH
-
-    def out_copy(step, slot):
-        return pltpu.make_async_copy(
-            buf.at[slot],
-            camgrad_o.at[:, pl.ds(pl.multiple_of(step * BLOCK, BLOCK), BLOCK), :],
-            sem.at[slot],
-        )
-
-    def body(step, carry):
-        slot = step & 1
-
-        @pl.when(step >= 2)
-        def _():
-            out_copy(step - 2, slot).wait()
-
-        tab = table[...]
-        blocks = []
-        for k in range(chunks):
-            at = pl.multiple_of((step * chunks + k) * ch_rows, ch_rows)
-            rows = pl.ds(at, ch_rows)
-            g = lax.dot_general(
-                feats[rows, :], tab, (((1,), (1,)), ((), ())), preferred_element_type=jnp.float32
-            ).astype(jnp.bfloat16)
-            direct = jnp.dot(amat[rows, :], tab, preferred_element_type=jnp.float32)
-            gp = jnp.concatenate(
-                [
-                    jnp.dot(
-                        g[c * height : (c + 1) * height],
-                        pick_of(row_id, codes, (step * chunks + k) * CH + c),
-                        preferred_element_type=jnp.float32,
-                    )
-                    for c in range(CH)
-                ],
-                axis=0,
+    tab = table[...]
+    wide = BLOCK * height
+    for step in range(steps):
+        rows = pl.ds(step * wide, wide)
+        g = lax.dot_general(
+            feats[rows, :], tab, (((1,), (1,)), ((), ())), preferred_element_type=jnp.float32
+        ).astype(jnp.bfloat16)
+        direct = jnp.dot(amat[rows, :], tab, preferred_element_type=jnp.float32)
+        gp = []
+        for c in range(0, BLOCK, 2):
+            both = jnp.dot(
+                g[c * height : (c + 2) * height],
+                picks[(step * BLOCK + c) // 2],
+                preferred_element_type=jnp.float32,
             )
-            mean = jnp.sum(gp * probs[rows, :], axis=1, keepdims=True)
-            gl = ((gp - mean) * slope[rows, :]).astype(jnp.bfloat16)
-            depth = jnp.dot(gl, wdp[...], preferred_element_type=jnp.float32)
-            blocks.append((direct + depth).astype(jnp.bfloat16))
-        block = jnp.concatenate(blocks, axis=0)
+            gp.append(both[:height, :lanes])
+            gp.append(both[height:, lanes:])
+        gp = jnp.concatenate(gp, axis=0)
+        mean = jnp.sum(gp * probs[rows, :], axis=1, keepdims=True)
+        gl = ((gp - mean) * slope[rows, :]).astype(jnp.bfloat16)
+        depth = jnp.dot(gl, wdp[...], preferred_element_type=jnp.float32)
+        block = (direct + depth).astype(jnp.bfloat16)
         for h0 in range(0, height, BLOCK):
             part = jnp.concatenate(
                 [block[c * height + h0 : c * height + h0 + BLOCK] for c in range(BLOCK)], axis=0
             )
             turned = jnp.dot(turn, part, preferred_element_type=jnp.float32)
-            buf[slot, h0 : h0 + BLOCK, :, :] = turned.astype(jnp.bfloat16).reshape(
-                BLOCK, BLOCK, -1
-            )
-        out_copy(step, slot).start()
-        return carry
-
-    lax.fori_loop(0, steps, body, 0)
-    for k in (2, 1):
-        out_copy(steps - k, (steps - k) & 1).wait()
-    for copy in small:
+            buf[h0 : h0 + BLOCK, pl.ds(step * BLOCK, BLOCK), :] = turned.astype(
+                jnp.bfloat16
+            ).reshape(BLOCK, BLOCK, -1)
+        done = pl.ds(step * BLOCK, BLOCK)
+        copy = pltpu.make_async_copy(buf.at[:, done, :], camgrad_o.at[:, done, :], sem.at[step])
+        copy.start()
+        copies.append(copy)
+    for copy in copies:
         copy.wait()
 
 
@@ -444,13 +406,13 @@
     rows = cols * height
     turned_counts = pillar_counts.T
     turned_depth = depth_weight.T
-    merged, lid_grad, table, codes, feats, amat, probs, slope = pl.pallas_call(
+    merged, lid_grad, table, picks, feats, amat, probs, slope = pl.pallas_call(
         functools.partial(kernel, n, strips, cols, height, br, ba, bins_n),
         out_shape=(
             pltpu.VMEM((br, ba, cf), bf),
             pltpu.VMEM((br, ba, cl), bf),
             pltpu.VMEM((groups, channels), bf),
-            pltpu.VMEM((cols, lanes), f32),
+            pltpu.VMEM((cols // 2, groups, 2 * lanes), bf),
             pltpu.VMEM((rows, channels), bf),
             pltpu.VMEM((rows, groups), bf),
             pltpu.VMEM((rows, lanes), f32),
@@ -475,7 +437,8 @@
             pltpu.VMEM((cols * height, 1), f32),
             pltpu.VMEM((cols * height, lanes), bf),
             pltpu.VMEM((groups, lanes), bf),
-            pltpu.VMEM((groups, channels), f32),
+            pltpu.VMEM((cols, lanes), f32),
+            pltpu.VMEM((cols, lanes, groups), bf),
             pltpu.VMEM((used, channels), bf),
             pltpu.VMEM((n1, channels), bf),
             pltpu.VMEM((n2, channels), bf),
@@ -491,7 +454,7 @@
             pltpu.SemaphoreType.DMA((16,)),
         ],
         compiler_params=pltpu.CompilerParams(
-            collective_id=0, has_side_effects=True, vmem_limit_bytes=40 * 1024 * 1024
+            collective_id=0, has_side_effects=True, vmem_limit_bytes=44 * 1024 * 1024
         ),
         name="bev",
     )(
@@ -515,13 +478,12 @@
         out_specs=(hbm,) * 3,
         scratch_shapes=[
             pltpu.VMEM((lanes, channels), bf),
-            pltpu.VMEM((groups, lanes), bf),
-            pltpu.VMEM((2, height, BLOCK, channels), bf),
-            pltpu.SemaphoreType.DMA((4,)),
+            pltpu.VMEM((height, cols, channels), bf),
+            pltpu.SemaphoreType.DMA((steps + 2,)),
         ],
-        compiler_params=pltpu.CompilerParams(vmem_limit_bytes=40 * 1024 * 1024),
+        compiler_params=pltpu.CompilerParams(vmem_limit_bytes=20 * 1024 * 1024),
         name="back",
-    )(feats, amat, probs, slope, codes, table, turned_depth, merged, lid_grad)
+    )(feats, amat, probs, slope, picks, table, turned_depth, merged, lid_grad)
     return merged, cam_grad, lid_grad
 
 

time: 37.3 us -> 31.1 us (0.83)
  Pallas kernels: 36.5 us -> 30.2 us
    pallas_call x1, Pallas kernels: 30.3 us -> 25.9 us  [local(): pl.pallas_call(functools.partial(kernel, n, strips, cols, height, br, ba,...]
    pallas_call x1, Pallas kernels: 6.24 us -> 4.36 us  [local(): pl.pallas_call(functools.partial(back_kernel, height, bins_n, steps), out...]
where the time goes in v2:
time: 31.1 us; the launch traced here: 30.9 us
  Pallas kernels  30.2 us (97%)
  between operations  0.66 us (2%)
    pallas_call x1, Pallas kernels, local(): pl.pallas_call(functools.partial(kernel, n, strips, cols, height, br, ba,...  25.9 us
    pallas_call x1, Pallas kernels, local(): pl.pallas_call(functools.partial(back_kernel, height, bins_n, steps), out...  4.36 us

profile of v2, /device:TPU:0, one launch (start us, length us, event | category | flops | bytes accessed | tf_op | source)
XLA Modules:
  0.0 30.9 jit_solution(11296306761705295972)
XLA Ops:
  0.6 0.0 copy-start
  0.6 25.9 %bev.1 = (bf16[16,4,256]{2,1,0:T(4,128)(2,1)S(1)}, bf16[16,4,128]{2,1,0:T(4,128)(2,1)S(1)}, bf16[192,256]{1,0:T(8,128)(2,1)S(1)}, bf16[32,192,256]{2,1,0:T(8,128...) custom-call(bf16[32,64,256]{2,1,0:T(8,128)(2,1)} %img_hbm.1, ...), custom_call_target="tpu_custom_call" | custom-call | tf_op jit(solution)/shard_map/bev/pallas_call | solution.py:409
  26.5 0.0 copy-done
  26.6 4.4 %back.1 = (bf16[32,64,256]{2,1,0:T(8,128)(2,1)}, bf16[16,4,256]{2,1,0:T(4,128)(2,1)}, bf16[16,4,128]{2,1,0:T(4,128)(2,1)}) custom-call(bf16[2048,256]{1,0:T(8,128)(2,1)S(1)} %get-tuple-element.14.feats, bf16[2048,192]{1,0:T(8,128)(2,1)S(1)} %get-tuple-element.15.amat, f32[2048,128]{1,0:T(8,128)S(1)} %get-tuple-element.16.probs, ...), custom_call_target="tpu_custom_call" | custom-call | tf_op jit(solution)/shard_map/back/pallas_call | solution.py:470
Async XLA Ops:
  0.6 25.9 %copy-start = (bf16[256,118]{0,1:T(8,128)(2,1)S(1)}, bf16[256,118]{0,1:T(8,128)(2,1)}, u32[]{:S(2)}) copy-start(bf16[256,118]{0,1:T(8,128)(2,1)} %param.11) | copy-start | bytes 181252

commit v3 on v2

--- a/solution.py
+++ b/solution.py
@@ -76,7 +76,7 @@
     img, cw, mw, xin, y1, y2, wd, bins, pillars, counts, lw, cot,
     wdp, sums, low, row_id, codes, routes, sendbuf,
     rp1, rp2, rp3, rm1, rm2, rm3, win, lidwin, cotwin,
-    local_sem, send_sem, recv_sem,
+    local_sem, image_sem, send_sem, recv_sem,
 ):
     me = lax.axis_index(AXES[0]) * strips + lax.axis_index(AXES[1])
     ch_rows = CH * height
@@ -92,8 +92,19 @@
             barrier, inc=1, device_id=dev(d), device_id_type=pl.DeviceIdType.MESH
         )
     layers = cw.shape[0]
+    blocks = range(0, height, BLOCK)
+    chunks = [
+        pltpu.make_async_copy(
+            img_hbm.at[pl.ds(h0, BLOCK)], img.at[pl.ds(h0, BLOCK)], image_sem.at[i]
+        )
+        for i, h0 in enumerate(blocks)
+    ]
+    fetches = [
+        pltpu.make_async_copy(cw_hbm.at[k], cw.at[k], local_sem.at[k]) for k in range(layers)
+    ]
+    fetches.append(pltpu.make_async_copy(mw_hbm, mw, local_sem.at[layers]))
     small = [
-        pltpu.make_async_copy(src, dst, local_sem.at[layers + 2 + i])
+        pltpu.make_async_copy(src, dst, local_sem.at[layers + 1 + i])
         for i, (src, dst) in enumerate(
             (
                 (bins_hbm, bins), (pillars_hbm, pillars), (counts_hbm, counts), (lw_hbm, lw),
@@ -101,21 +112,14 @@
             )
         )
     ]
-    for copy in small:
+    for copy in (small[0], *chunks, fetches[0], *small[1:]):
         copy.start()
-    image = pltpu.make_async_copy(img_hbm, img, local_sem.at[layers + 1])
-    image.start()
-    fetches = [
-        pltpu.make_async_copy(cw_hbm.at[k], cw.at[k], local_sem.at[k]) for k in range(layers)
-    ]
-    fetches.append(pltpu.make_async_copy(mw_hbm, mw, local_sem.at[layers]))
-    for copy in fetches:
-        copy.start()
-
     row_id[...] = row_numbers(row_id.shape)
     wdp[...] = jnp.zeros_like(wdp)
     codes[...] = jnp.full(codes.shape, -1.0, jnp.float32)
     win[...] = jnp.zeros_like(win)
+    sec = ba * br
+    cot_own, lid_own = (ba + 1) * br, (ba + 2) * br
     small[0].wait()
     cell = br * ba
     sh_cell, sh_ba, sh_br = cell.bit_length() - 1, ba.bit_length() - 1, br.bit_length() - 1
@@ -127,64 +131,37 @@
     code = (((off << sh_ba) + (in_cell & (ba - 1))) << sh_br) + (in_cell >> sh_ba)
     codes[:, 0:bins_n] = code.astype(jnp.float32)
     turned_codes = jnp.transpose(codes[...])
-    cells = lax.broadcasted_iota(jnp.int32, routes.shape[1:], 1)
-    cells = cells.astype(jnp.float32).astype(jnp.bfloat16)
-    for j in range(cols):
-        code = jnp.broadcast_to(turned_codes[:, j : j + 1], cells.shape).astype(jnp.bfloat16)
-        routes[j] = one_hot(code == cells)
-    for copy in small[1:]:
+    turn = block_turn()
+    for copy, h0 in zip(chunks, blocks):
         copy.wait()
-    sec = ba * br
-    cot_own, lid_own = (ba + 1) * br, (ba + 2) * br
-    cot_f = cot[...].astype(jnp.float32)
-    for a in range(ba):
-        cotwin[pl.ds(cot_own + a * br, br), :] = cot_f[:, a, :].astype(jnp.bfloat16)
-    points = counts[...]
-    scale = (points > 0).astype(jnp.float32) / jnp.maximum(points, 1).astype(jnp.float32)
-    pil = pillars[...].astype(jnp.float32)
-    pil = jnp.concatenate(
-        [pil[k] * scale[:, k : k + 1] for k in range(2 * br)], axis=0
-    ).astype(jnp.bfloat16)
-    lb, la = br.bit_length() - 1, ba.bit_length() - 1
-
-    def pillar_row(p):
-        r, a, uv = p & (br - 1), (p >> lb) & (ba - 1), p >> (lb + la)
-        return ((2 * r + (uv >> 1)) << (la + 1)) + 2 * a + (uv & 1)
-
-    gathered = jnp.dot(
-        one_hot_rows(4 * sec, 4 * sec, pillar_row), pil, preferred_element_type=jnp.float32
-    ).astype(jnp.bfloat16)
-    taps = jnp.concatenate([gathered[k * sec : (k + 1) * sec] for k in range(4)], axis=1)
-    lid = jnp.dot(
-        taps, lw[...].reshape(taps.shape[1], -1), preferred_element_type=jnp.float32
-    )
-    lidwin[pl.ds(lid_own, sec), :] = jnp.maximum(lid, 0.0).astype(jnp.bfloat16)
-
-    wdp[0:bins_n, :] = wd[...]
-    image.wait()
-    turn = block_turn()
-    for j0 in range(0, cols, BLOCK):
-        for h0 in range(0, height, BLOCK):
+        for j0 in range(0, cols, BLOCK):
             block = img[h0 : h0 + BLOCK, j0 : j0 + BLOCK, :].reshape(BLOCK * BLOCK, -1)
             turned = jnp.dot(turn, block, preferred_element_type=jnp.float32)
             turned = turned.astype(jnp.bfloat16)
             for c in range(BLOCK):
                 at = (3 + j0 + c) * height + h0
                 xin[pl.ds(at, BLOCK), :] = turned[c * BLOCK : (c + 1) * BLOCK]
+    for copy in fetches[1:]:
+        copy.start()
     fetches[0].wait()
 
-    def interior(src, dst, layer, first, shift, count, wide):
-        def step(i, carry):
-            c = jnp.minimum(first + wide * i, cols - first - wide) + shift
-            at = pl.multiple_of(c * height, height)
-            size = wide * height
+    cells = lax.broadcasted_iota(jnp.int32, routes.shape[1:], 1)
+    cells = cells.astype(jnp.float32).astype(jnp.bfloat16)
+
+    def route(j):
+        code = jnp.broadcast_to(turned_codes[:, j : j + 1], cells.shape).astype(jnp.bfloat16)
+        routes[j] = one_hot(code == cells)
+
+    def interior(src, dst, layer, first, last, beside=None):
+        for c in range(first, last, 4 * CH):
+            if beside is not None:
+                for j in range(c - first, min(c - first + 4 * CH, cols)):
+                    beside(j)
+            at, size = c * height, (min(c + 4 * CH, last) - c) * height
             dst[pl.ds(at, size), :] = conv_rows(src, [(at, size)], cw, layer, height)
-            return carry
-
-        lax.fori_loop(0, count, step, 0)
 
     full = cols // CH
-    interior(xin, y1, 0, 1, 2, full // 2, 2 * CH)
+    interior(xin, y1, 0, 3, cols + 1, route)
     pl.semaphore_wait(barrier, 6)
 
     messages = []
@@ -205,7 +182,14 @@
     h3 = 3 * height
     send(xin.at[pl.ds(cols * height, h3)], xin.at[pl.ds(0, h3)], 1)
     send(xin.at[pl.ds(h3, h3)], xin.at[pl.ds((cols + 3) * height, h3)], -1)
-    for window, start, edge in ((cotwin, cot_own, br), (lidwin, lid_own, 2 * br)):
+    for copy in small[1:]:
+        copy.wait()
+    wdp[0:bins_n, :] = wd[...]
+    cot_f = cot[...].astype(jnp.float32)
+    for a in range(ba):
+        cotwin[pl.ds(cot_own + a * br, br), :] = cot_f[:, a, :].astype(jnp.bfloat16)
+
+    def spread(window, start, edge):
         mine = window.at[pl.ds(start, sec)]
         send(mine, window.at[pl.ds(edge, sec)], 1)
         send(mine, window.at[pl.ds(start + sec, sec)], -1)
@@ -213,22 +197,53 @@
         send(last, window.at[pl.ds(0, edge)], 2)
         send(window.at[pl.ds(start, edge)], window.at[pl.ds(start + 2 * sec, edge)], -2)
 
+    spread(cotwin, cot_own, br)
+
     fetches[1].wait()
-    interior(y1, y2, 1, 2, 1, full // 2, 2 * CH)
+    interior(y1, y2, 1, 3, cols - 1)
     fetches[2].wait()
-    interior(y2, feats, 2, 3, 0, full // 2 - 1, 2 * CH)
-
     messages[0].wait_recv()
     messages[1].wait_recv()
-    for layer, (src, dst, extra, done) in enumerate(
-        ((xin, y1, 4, cols - 2), (y1, y2, 2, cols - 4), (y2, feats, 0, cols - 2 * CH))
-    ):
+
+    def edge(layer, src, dst, extra, done):
         right = (3 + done) * height
         size = (cols + extra) * height - right
-        edge = conv_rows(src, [(0, h3), (right, size)], cw, layer, height)
-        dst[pl.ds(0, h3), :] = edge[:h3]
-        dst[pl.ds(right, size), :] = edge[h3:]
-
+        both = conv_rows(src, [(0, h3), (right, size)], cw, layer, height)
+        dst[pl.ds(0, h3), :] = both[:h3]
+        dst[pl.ds(right, size), :] = both[h3:]
+
+    def middle(i):
+        at, size = (3 + 2 * CH * i) * height, 2 * CH * height
+        feats[pl.ds(at, size), :] = conv_rows(y2, [(at, size)], cw, 2, height)
+
+    inner = full // 2 - 1
+    edge(0, xin, y1, 4, cols - 2)
+    for i in range(inner):
+        middle(i)
+        if i == 0:
+            points = counts[...]
+            scale = (points > 0).astype(jnp.float32) / jnp.maximum(points, 1).astype(jnp.float32)
+            pil = pillars[...].astype(jnp.float32)
+            pil = jnp.concatenate(
+                [pil[k] * scale[:, k : k + 1] for k in range(2 * br)], axis=0
+            ).astype(jnp.bfloat16)
+            lb, la = br.bit_length() - 1, ba.bit_length() - 1
+
+            def pillar_row(p):
+                r, a, uv = p & (br - 1), (p >> lb) & (ba - 1), p >> (lb + la)
+                return ((2 * r + (uv >> 1)) << (la + 1)) + 2 * a + (uv & 1)
+
+            gathered = jnp.dot(
+                one_hot_rows(4 * sec, 4 * sec, pillar_row), pil, preferred_element_type=jnp.float32
+            ).astype(jnp.bfloat16)
+            taps = jnp.concatenate([gathered[k * sec : (k + 1) * sec] for k in range(4)], axis=1)
+            lid = jnp.dot(
+                taps, lw[...].reshape(taps.shape[1], -1), preferred_element_type=jnp.float32
+            )
+            lidwin[pl.ds(lid_own, sec), :] = jnp.maximum(lid, 0.0).astype(jnp.bfloat16)
+            edge(1, y1, y2, 2, cols - 4)
+    edge(2, y2, feats, 0, cols - 2 * CH)
+    spread(lidwin, lid_own, 2 * br)
     used = 3 * ba * br
     wide = 2 * CH * height
     lane = lax.broadcasted_iota(jnp.int32, (wide, lanes), 1)
@@ -336,12 +351,12 @@
     height, bins_n, steps,
     feats, amat, probs, slope, picks, table, wd, merged, lid_grad,
     camgrad_o, merged_o, lidgrad_o,
-    wdp, buf, sem,
+    wdp, seen, gprobs, buf, sem,
 ):
     lanes = wdp.shape[0]
     copies = [
-        pltpu.make_async_copy(merged, merged_o, sem.at[steps]),
-        pltpu.make_async_copy(lid_grad, lidgrad_o, sem.at[steps + 1]),
+        pltpu.make_async_copy(merged, merged_o, sem.at[0]),
+        pltpu.make_async_copy(lid_grad, lidgrad_o, sem.at[1]),
     ]
     for copy in copies:
         copy.start()
@@ -349,39 +364,37 @@
     wdp[0:bins_n, :] = wd[...]
     turn = block_turn()
     tab = table[...]
+    seen[...] = lax.dot_general(
+        feats[...], tab, (((1,), (1,)), ((), ())), preferred_element_type=jnp.float32
+    ).astype(jnp.bfloat16)
+    for pair in range(picks.shape[0]):
+        at = 2 * pair * height
+        both = jnp.dot(
+            seen[pl.ds(at, 2 * height), :], picks[pair], preferred_element_type=jnp.float32
+        )
+        gprobs[pl.ds(at, height), :] = both[:height, :lanes]
+        gprobs[pl.ds(at + height, height), :] = both[height:, lanes:]
     wide = BLOCK * height
     for step in range(steps):
         rows = pl.ds(step * wide, wide)
-        g = lax.dot_general(
-            feats[rows, :], tab, (((1,), (1,)), ((), ())), preferred_element_type=jnp.float32
-        ).astype(jnp.bfloat16)
-        direct = jnp.dot(amat[rows, :], tab, preferred_element_type=jnp.float32)
-        gp = []
-        for c in range(0, BLOCK, 2):
-            both = jnp.dot(
-                g[c * height : (c + 2) * height],
-                picks[(step * BLOCK + c) // 2],
-                preferred_element_type=jnp.float32,
-            )
-            gp.append(both[:height, :lanes])
-            gp.append(both[height:, lanes:])
-        gp = jnp.concatenate(gp, axis=0)
+        gp = gprobs[rows, :]
         mean = jnp.sum(gp * probs[rows, :], axis=1, keepdims=True)
         gl = ((gp - mean) * slope[rows, :]).astype(jnp.bfloat16)
+        direct = jnp.dot(amat[rows, :], tab, preferred_element_type=jnp.float32)
         depth = jnp.dot(gl, wdp[...], preferred_element_type=jnp.float32)
         block = (direct + depth).astype(jnp.bfloat16)
-        for h0 in range(0, height, BLOCK):
+        for k, h0 in enumerate(range(0, height, BLOCK)):
             part = jnp.concatenate(
                 [block[c * height + h0 : c * height + h0 + BLOCK] for c in range(BLOCK)], axis=0
             )
             turned = jnp.dot(turn, part, preferred_element_type=jnp.float32)
-            buf[h0 : h0 + BLOCK, pl.ds(step * BLOCK, BLOCK), :] = turned.astype(
-                jnp.bfloat16
-            ).reshape(BLOCK, BLOCK, -1)
-        done = pl.ds(step * BLOCK, BLOCK)
-        copy = pltpu.make_async_copy(buf.at[:, done, :], camgrad_o.at[:, done, :], sem.at[step])
-        copy.start()
-        copies.append(copy)
+            spot = (pl.ds(h0, BLOCK), pl.ds(step * BLOCK, BLOCK))
+            buf[spot] = turned.astype(jnp.bfloat16).reshape(BLOCK, BLOCK, -1)
+            copy = pltpu.make_async_copy(
+                buf.at[spot], camgrad_o.at[spot], sem.at[2 + step * (height // BLOCK) + k]
+            )
+            copy.start()
+            copies.append(copy)
     for copy in copies:
         copy.wait()
 
@@ -449,7 +462,8 @@
             pltpu.VMEM((total, channels), f32),
             pltpu.VMEM((total, cl), bf),
             pltpu.VMEM((total - 2 * br, cf), bf),
-            pltpu.SemaphoreType.DMA((cam_weights.shape[0] + 8,)),
+            pltpu.SemaphoreType.DMA((cam_weights.shape[0] + 7,)),
+            pltpu.SemaphoreType.DMA((height // BLOCK,)),
             pltpu.SemaphoreType.DMA((16,)),
             pltpu.SemaphoreType.DMA((16,)),
         ],
@@ -478,8 +492,10 @@
         out_specs=(hbm,) * 3,
         scratch_shapes=[
             pltpu.VMEM((lanes, channels), bf),
+            pltpu.VMEM((rows, groups), bf),
+            pltpu.VMEM((rows, lanes), f32),
             pltpu.VMEM((height, cols, channels), bf),
-            pltpu.SemaphoreType.DMA((steps + 2,)),
+            pltpu.SemaphoreType.DMA((2 + steps * (height // BLOCK),)),
         ],
         compiler_params=pltpu.CompilerParams(vmem_limit_bytes=20 * 1024 * 1024),
         name="back",

time: 31.1 us -> 28.6 us (0.920)
  Pallas kernels: 30.2 us -> 27.8 us
    pallas_call x1, Pallas kernels: 25.9 us -> 24 us  [local(): pl.pallas_call(functools.partial(kernel, n, strips, cols, height, br, ba,...]
    pallas_call x1, Pallas kernels: 4.36 us -> 3.86 us  [local(): pl.pallas_call(functools.partial(back_kernel, height, bins_n, steps), out...]
where the time goes in v3:
time: 28.6 us; the launch traced here: 28.5 us
  Pallas kernels  27.8 us (97%)
  between operations  0.66 us (2%)
    pallas_call x1, Pallas kernels, local(): pl.pallas_call(functools.partial(kernel, n, strips, cols, height, br, ba,...  24 us
    pallas_call x1, Pallas kernels, local(): pl.pallas_call(functools.partial(back_kernel, height, bins_n, steps), out...  3.86 us

profile of v3, /device:TPU:0, one launch (start us, length us, event | category | flops | bytes accessed | tf_op | source)
XLA Modules:
  0.0 28.5 jit_solution(14313694483822267646)
XLA Ops:
  0.6 0.0 copy-start
  0.6 24.0 %bev.1 = (bf16[16,4,256]{2,1,0:T(4,128)(2,1)S(1)}, bf16[16,4,128]{2,1,0:T(4,128)(2,1)S(1)}, bf16[192,256]{1,0:T(8,128)(2,1)S(1)}, bf16[32,192,256]{2,1,0:T(8,128...) custom-call(bf16[32,64,256]{2,1,0:T(8,128)(2,1)} %img_hbm.1, ...), custom_call_target="tpu_custom_call" | custom-call | tf_op jit(solution)/shard_map/bev/pallas_call | solution.py:422
  24.6 0.0 copy-done
  24.6 3.9 %back.1 = (bf16[32,64,256]{2,1,0:T(8,128)(2,1)}, bf16[16,4,256]{2,1,0:T(4,128)(2,1)}, bf16[16,4,128]{2,1,0:T(4,128)(2,1)}) custom-call(bf16[2048,256]{1,0:T(8,128)(2,1)S(1)} %get-tuple-element.14.feats, bf16[2048,192]{1,0:T(8,128)(2,1)S(1)} %get-tuple-element.15.amat, f32[2048,128]{1,0:T(8,128)S(1)} %get-tuple-element.16.probs, ...), custom_call_target="tpu_custom_call" | custom-call | tf_op jit(solution)/shard_map/back/pallas_call | solution.py:484
Async XLA Ops:
  0.6 24.0 %copy-start = (bf16[256,118]{0,1:T(8,128)(2,1)S(1)}, bf16[256,118]{0,1:T(8,128)(2,1)}, u32[]{:S(2)}) copy-start(bf16[256,118]{0,1:T(8,128)(2,1)} %param.11) | copy-start | bytes 181252

commit v4 on v3

--- a/solution.py
+++ b/solution.py
@@ -93,11 +93,10 @@
         )
     layers = cw.shape[0]
     blocks = range(0, height, BLOCK)
+    half = BLOCK // 2
     chunks = [
-        pltpu.make_async_copy(
-            img_hbm.at[pl.ds(h0, BLOCK)], img.at[pl.ds(h0, BLOCK)], image_sem.at[i]
-        )
-        for i, h0 in enumerate(blocks)
+        pltpu.make_async_copy(img_hbm.at[pl.ds(h0, half)], img.at[pl.ds(h0, half)], image_sem.at[i])
+        for i, h0 in enumerate(range(0, height, half))
     ]
     fetches = [
         pltpu.make_async_copy(cw_hbm.at[k], cw.at[k], local_sem.at[k]) for k in range(layers)
@@ -112,7 +111,7 @@
             )
         )
     ]
-    for copy in (small[0], *chunks, fetches[0], *small[1:]):
+    for copy in (*chunks, small[0], fetches[0]):
         copy.start()
     row_id[...] = row_numbers(row_id.shape)
     wdp[...] = jnp.zeros_like(wdp)
@@ -132,8 +131,9 @@
     codes[:, 0:bins_n] = code.astype(jnp.float32)
     turned_codes = jnp.transpose(codes[...])
     turn = block_turn()
-    for copy, h0 in zip(chunks, blocks):
-        copy.wait()
+    for i, h0 in enumerate(blocks):
+        chunks[2 * i].wait()
+        chunks[2 * i + 1].wait()
         for j0 in range(0, cols, BLOCK):
             block = img[h0 : h0 + BLOCK, j0 : j0 + BLOCK, :].reshape(BLOCK * BLOCK, -1)
             turned = jnp.dot(turn, block, preferred_element_type=jnp.float32)
@@ -141,7 +141,7 @@
             for c in range(BLOCK):
                 at = (3 + j0 + c) * height + h0
                 xin[pl.ds(at, BLOCK), :] = turned[c * BLOCK : (c + 1) * BLOCK]
-    for copy in fetches[1:]:
+    for copy in (*small[1:], *fetches[1:]):
         copy.start()
     fetches[0].wait()
 
@@ -247,7 +247,8 @@
     used = 3 * ba * br
     wide = 2 * CH * height
     lane = lax.broadcasted_iota(jnp.int32, (wide, lanes), 1)
-    for at in range(0, cols * height, wide):
+
+    def soften(at):
         rows = pl.ds(at, wide)
         logits = lax.dot_general(
             feats[rows, :], wdp[...], (((1,), (1,)), ((), ())), preferred_element_type=jnp.float32
@@ -261,22 +262,29 @@
         slope[rows, :] = logits
         sums[rows, :] = inv
         low[rows, :] = p.astype(jnp.bfloat16)
-    for j in range(cols):
-        rows = pl.ds(j * height, height)
-        a = jnp.dot(low[rows, :], routes[j], preferred_element_type=jnp.float32)
-        amat[rows, :] = a.astype(jnp.bfloat16)
+
+    def lift(at):
+        for row in range(at, at + wide, height):
+            rows = pl.ds(row, height)
+            a = jnp.dot(low[rows, :], routes[row // height], preferred_element_type=jnp.float32)
+            amat[rows, :] = a.astype(jnp.bfloat16)
+
+    soften(0)
+    for at in range(0, cols * height, wide):
+        if at + wide < cols * height:
+            soften(at + wide)
+        lift(at)
     mine = lax.dot_general(
         amat[...], feats[...], (((0,), (0,)), ((), ())), preferred_element_type=jnp.float32
     )
     sendbuf[...] = mine.astype(jnp.bfloat16)
     n1, n2, n3 = (2 * ba + 2) * br, (ba + 2) * br, 2 * br
+    send(sendbuf.at[pl.ds(used - n3, n3)], rp3, 3)
+    send(sendbuf.at[pl.ds(0, n3)], rm3, -3)
+    send(sendbuf.at[pl.ds(used - n2, n2)], rp2, 2)
+    send(sendbuf.at[pl.ds(0, n2)], rm2, -2)
     send(sendbuf.at[pl.ds(used - n1, n1)], rp1, 1)
     send(sendbuf.at[pl.ds(0, n1)], rm1, -1)
-    send(sendbuf.at[pl.ds(used - n2, n2)], rp2, 2)
-    send(sendbuf.at[pl.ds(0, n2)], rm2, -2)
-    send(sendbuf.at[pl.ds(used - n3, n3)], rp3, 3)
-    send(sendbuf.at[pl.ds(0, n3)], rm3, -3)
-
     for at in range(0, cols * height, wide):
         rows = pl.ds(at, wide)
         sig = jax.nn.sigmoid(slope[rows, :]) * sums[rows, :]
@@ -351,7 +359,7 @@
     height, bins_n, steps,
     feats, amat, probs, slope, picks, table, wd, merged, lid_grad,
     camgrad_o, merged_o, lidgrad_o,
-    wdp, seen, gprobs, buf, sem,
+    wdp, seen, gprobs, glog, buf, sem,
 ):
     lanes = wdp.shape[0]
     copies = [
@@ -374,24 +382,31 @@
         )
         gprobs[pl.ds(at, height), :] = both[:height, :lanes]
         gprobs[pl.ds(at + height, height), :] = both[height:, lanes:]
+    gp = gprobs[...]
+    mean = jnp.sum(gp * probs[...], axis=1, keepdims=True)
+    glog[...] = ((gp - mean) * slope[...]).astype(jnp.bfloat16)
     wide = BLOCK * height
-    for step in range(steps):
+
+    def total(step):
         rows = pl.ds(step * wide, wide)
-        gp = gprobs[rows, :]
-        mean = jnp.sum(gp * probs[rows, :], axis=1, keepdims=True)
-        gl = ((gp - mean) * slope[rows, :]).astype(jnp.bfloat16)
         direct = jnp.dot(amat[rows, :], tab, preferred_element_type=jnp.float32)
-        depth = jnp.dot(gl, wdp[...], preferred_element_type=jnp.float32)
-        block = (direct + depth).astype(jnp.bfloat16)
-        for k, h0 in enumerate(range(0, height, BLOCK)):
+        depth = jnp.dot(glog[rows, :], wdp[...], preferred_element_type=jnp.float32)
+        return (direct + depth).astype(jnp.bfloat16)
+
+    blocks = [total(step) for step in range(steps)]
+    for k, h0 in enumerate(range(0, height, BLOCK)):
+        for step, block in enumerate(blocks):
             part = jnp.concatenate(
                 [block[c * height + h0 : c * height + h0 + BLOCK] for c in range(BLOCK)], axis=0
             )
             turned = jnp.dot(turn, part, preferred_element_type=jnp.float32)
-            spot = (pl.ds(h0, BLOCK), pl.ds(step * BLOCK, BLOCK))
-            buf[spot] = turned.astype(jnp.bfloat16).reshape(BLOCK, BLOCK, -1)
+            buf[h0 : h0 + BLOCK, pl.ds(step * BLOCK, BLOCK), :] = turned.astype(
+                jnp.bfloat16
+            ).reshape(BLOCK, BLOCK, -1)
+        for q in range(4):
+            rows = pl.ds(h0 + q * (BLOCK // 4), BLOCK // 4)
             copy = pltpu.make_async_copy(
-                buf.at[spot], camgrad_o.at[spot], sem.at[2 + step * (height // BLOCK) + k]
+                buf.at[rows], camgrad_o.at[rows], sem.at[2 + 4 * k + q]
             )
             copy.start()
             copies.append(copy)
@@ -463,7 +478,7 @@
             pltpu.VMEM((total, cl), bf),
             pltpu.VMEM((total - 2 * br, cf), bf),
             pltpu.SemaphoreType.DMA((cam_weights.shape[0] + 7,)),
-            pltpu.SemaphoreType.DMA((height // BLOCK,)),
+            pltpu.SemaphoreType.DMA((2 * height // BLOCK,)),
             pltpu.SemaphoreType.DMA((16,)),
             pltpu.SemaphoreType.DMA((16,)),
         ],
@@ -494,8 +509,9 @@
             pltpu.VMEM((lanes, channels), bf),
             pltpu.VMEM((rows, groups), bf),
             pltpu.VMEM((rows, lanes), f32),
+            pltpu.VMEM((rows, lanes), bf),
             pltpu.VMEM((height, cols, channels), bf),
-            pltpu.SemaphoreType.DMA((2 + steps * (height // BLOCK),)),
+            pltpu.SemaphoreType.DMA((2 + 4 * (height // BLOCK),)),
         ],
         compiler_params=pltpu.CompilerParams(vmem_limit_bytes=20 * 1024 * 1024),
         name="back",

time: 28.6 us -> 28.2 us (0.986)
  Pallas kernels: 27.8 us -> 27.4 us
    pallas_call x1, Pallas kernels: 3.86 us -> 2.8 us  [local(): pl.pallas_call(functools.partial(back_kernel, height, bins_n, steps), out...]
    pallas_call x1, Pallas kernels: 24 us -> 24.6 us  [local(): pl.pallas_call(functools.partial(kernel, n, strips, cols, height, br, ba,...]
where the time goes in v4:
time: 28.2 us; the launch traced here: 28.1 us
  Pallas kernels  27.4 us (97%)
  between operations  0.66 us (2%)
    pallas_call x1, Pallas kernels, local(): pl.pallas_call(functools.partial(kernel, n, strips, cols, height, br, ba,...  24.6 us
    pallas_call x1, Pallas kernels, local(): pl.pallas_call(functools.partial(back_kernel, height, bins_n, steps), out...  2.8 us

profile of v4, /device:TPU:0, one launch (start us, length us, event | category | flops | bytes accessed | tf_op | source)
XLA Modules:
  0.0 28.1 jit_solution(14851626500136800797)
XLA Ops:
  0.6 0.0 copy-start
  0.6 24.6 %bev.1 = (bf16[16,4,256]{2,1,0:T(4,128)(2,1)S(1)}, bf16[16,4,128]{2,1,0:T(4,128)(2,1)S(1)}, bf16[192,256]{1,0:T(8,128)(2,1)S(1)}, bf16[32,192,256]{2,1,0:T(8,128...) custom-call(bf16[32,64,256]{2,1,0:T(8,128)(2,1)} %img_hbm.1, ...), custom_call_target="tpu_custom_call" | custom-call | tf_op jit(solution)/shard_map/bev/pallas_call | solution.py:437
  25.3 0.0 copy-done
  25.3 2.8 %back.1 = (bf16[32,64,256]{2,1,0:T(8,128)(2,1)}, bf16[16,4,256]{2,1,0:T(4,128)(2,1)}, bf16[16,4,128]{2,1,0:T(4,128)(2,1)}) custom-call(bf16[2048,256]{1,0:T(8,128)(2,1)S(1)} %get-tuple-element.14.feats, bf16[2048,192]{1,0:T(8,128)(2,1)S(1)} %get-tuple-element.15.amat, f32[2048,128]{1,0:T(8,128)S(1)} %get-tuple-element.16.probs, ...), custom_call_target="tpu_custom_call" | custom-call | tf_op jit(solution)/shard_map/back/pallas_call | solution.py:499
Async XLA Ops:
  0.6 24.7 %copy-start = (bf16[256,118]{0,1:T(8,128)(2,1)S(1)}, bf16[256,118]{0,1:T(8,128)(2,1)}, u32[]{:S(2)}) copy-start(bf16[256,118]{0,1:T(8,128)(2,1)} %param.11) | copy-start | bytes 181252

commit v5 on v4

--- a/solution.py
+++ b/solution.py
@@ -279,12 +279,12 @@
     )
     sendbuf[...] = mine.astype(jnp.bfloat16)
     n1, n2, n3 = (2 * ba + 2) * br, (ba + 2) * br, 2 * br
+    send(sendbuf.at[pl.ds(used - n1, n1)], rp1, 1)
+    send(sendbuf.at[pl.ds(0, n1)], rm1, -1)
+    send(sendbuf.at[pl.ds(used - n2, n2)], rp2, 2)
+    send(sendbuf.at[pl.ds(0, n2)], rm2, -2)
     send(sendbuf.at[pl.ds(used - n3, n3)], rp3, 3)
     send(sendbuf.at[pl.ds(0, n3)], rm3, -3)
-    send(sendbuf.at[pl.ds(used - n2, n2)], rp2, 2)
-    send(sendbuf.at[pl.ds(0, n2)], rm2, -2)
-    send(sendbuf.at[pl.ds(used - n1, n1)], rp1, 1)
-    send(sendbuf.at[pl.ds(0, n1)], rm1, -1)
     for at in range(0, cols * height, wide):
         rows = pl.ds(at, wide)
         sig = jax.nn.sigmoid(slope[rows, :]) * sums[rows, :]

time: 28.2 us -> 27.4 us (0.972)
  Pallas kernels: 27.4 us -> 26.4 us
    pallas_call x1, Pallas kernels: 24.6 us -> 23.6 us  [local(): pl.pallas_call(functools.partial(kernel, n, strips, cols, height, br, ba,...]
where the time goes in v5:
time: 27.4 us; the launch traced here: 27.1 us
  Pallas kernels  26.4 us (96%)
  between operations  0.66 us (2%)
    pallas_call x1, Pallas kernels, local(): pl.pallas_call(functools.partial(kernel, n, strips, cols, height, br, ba,...  23.6 us
    pallas_call x1, Pallas kernels, local(): pl.pallas_call(functools.partial(back_kernel, height, bins_n, steps), out...  2.8 us

profile of v5, /device:TPU:0, one launch (start us, length us, event | category | flops | bytes accessed | tf_op | source)
XLA Modules:
  0.0 27.1 jit_solution(13340258770415359842)
XLA Ops:
  0.6 0.0 copy-start
  0.6 23.6 %bev.1 = (bf16[16,4,256]{2,1,0:T(4,128)(2,1)S(1)}, bf16[16,4,128]{2,1,0:T(4,128)(2,1)S(1)}, bf16[192,256]{1,0:T(8,128)(2,1)S(1)}, bf16[32,192,256]{2,1,0:T(8,128...) custom-call(bf16[32,64,256]{2,1,0:T(8,128)(2,1)} %img_hbm.1, ...), custom_call_target="tpu_custom_call" | custom-call | tf_op jit(solution)/shard_map/bev/pallas_call | solution.py:437
  24.3 0.0 copy-done
  24.3 2.8 %back.1 = (bf16[32,64,256]{2,1,0:T(8,128)(2,1)}, bf16[16,4,256]{2,1,0:T(4,128)(2,1)}, bf16[16,4,128]{2,1,0:T(4,128)(2,1)}) custom-call(bf16[2048,256]{1,0:T(8,128)(2,1)S(1)} %get-tuple-element.14.feats, bf16[2048,192]{1,0:T(8,128)(2,1)S(1)} %get-tuple-element.15.amat, f32[2048,128]{1,0:T(8,128)S(1)} %get-tuple-element.16.probs, ...), custom_call_target="tpu_custom_call" | custom-call | tf_op jit(solution)/shard_map/back/pallas_call | solution.py:499
Async XLA Ops:
  0.6 23.7 %copy-start = (bf16[256,118]{0,1:T(8,128)(2,1)S(1)}, bf16[256,118]{0,1:T(8,128)(2,1)}, u32[]{:S(2)}) copy-start(bf16[256,118]{0,1:T(8,128)(2,1)} %param.11) | copy-start | bytes 181252

commit v6 on v5

--- a/solution.py
+++ b/solution.py
@@ -204,6 +204,31 @@
     fetches[2].wait()
     messages[0].wait_recv()
     messages[1].wait_recv()
+    used = 3 * ba * br
+    wide = 2 * CH * height
+    lane = lax.broadcasted_iota(jnp.int32, (wide, lanes), 1)
+
+    def soften(at):
+        rows = pl.ds(at, wide)
+        logits = lax.dot_general(
+            feats[rows, :], wdp[...], (((1,), (1,)), ((), ())), preferred_element_type=jnp.float32
+        )
+        e = jnp.exp(-jnp.abs(logits))
+        soft = jnp.maximum(logits, 0.0) + jnp.log(1.0 + e) + 0.05
+        soft = jnp.where(lane < bins_n, soft, 0.0)
+        inv = 1.0 / jnp.sum(soft, axis=1, keepdims=True)
+        p = soft * inv
+        probs[rows, :] = p
+        slope[rows, :] = logits
+        sums[rows, :] = inv
+        low[rows, :] = p.astype(jnp.bfloat16)
+
+    def lift(at):
+        for row in range(at, at + wide, height):
+            rows = pl.ds(row, height)
+            a = jnp.dot(low[rows, :], routes[row // height], preferred_element_type=jnp.float32)
+            amat[rows, :] = a.astype(jnp.bfloat16)
+
 
     def edge(layer, src, dst, extra, done):
         right = (3 + done) * height
@@ -242,38 +267,18 @@
             )
             lidwin[pl.ds(lid_own, sec), :] = jnp.maximum(lid, 0.0).astype(jnp.bfloat16)
             edge(1, y1, y2, 2, cols - 4)
+        else:
+            soften(i * wide)
     edge(2, y2, feats, 0, cols - 2 * CH)
+    early = [i * wide for i in range(1, inner)]
+    late = [at for at in range(0, cols * height, wide) if at not in early]
+    for at in early:
+        lift(at)
+    for at in late:
+        soften(at)
+    for at in late:
+        lift(at)
     spread(lidwin, lid_own, 2 * br)
-    used = 3 * ba * br
-    wide = 2 * CH * height
-    lane = lax.broadcasted_iota(jnp.int32, (wide, lanes), 1)
-
-    def soften(at):
-        rows = pl.ds(at, wide)
-        logits = lax.dot_general(
-            feats[rows, :], wdp[...], (((1,), (1,)), ((), ())), preferred_element_type=jnp.float32
-        )
-        e = jnp.exp(-jnp.abs(logits))
-        soft = jnp.maximum(logits, 0.0) + jnp.log(1.0 + e) + 0.05
-        soft = jnp.where(lane < bins_n, soft, 0.0)
-        inv = 1.0 / jnp.sum(soft, axis=1, keepdims=True)
-        p = soft * inv
-        probs[rows, :] = p
-        slope[rows, :] = logits
-        sums[rows, :] = inv
-        low[rows, :] = p.astype(jnp.bfloat16)
-
-    def lift(at):
-        for row in range(at, at + wide, height):
-            rows = pl.ds(row, height)
-            a = jnp.dot(low[rows, :], routes[row // height], preferred_element_type=jnp.float32)
-            amat[rows, :] = a.astype(jnp.bfloat16)
-
-    soften(0)
-    for at in range(0, cols * height, wide):
-        if at + wide < cols * height:
-            soften(at + wide)
-        lift(at)
     mine = lax.dot_general(
         amat[...], feats[...], (((0,), (0,)), ((), ())), preferred_element_type=jnp.float32
     )

time: 27.4 us -> 27.6 us (level)
  no operation moved by 1% of the time
where the time goes in v6:
time: 27.6 us; the launch traced here: 27.3 us
  Pallas kernels  26.6 us (96%)
  between operations  0.66 us (2%)
    pallas_call x1, Pallas kernels, local(): pl.pallas_call(functools.partial(kernel, n, strips, cols, height, br, ba,...  23.8 us
    pallas_call x1, Pallas kernels, local(): pl.pallas_call(functools.partial(back_kernel, height, bins_n, steps), out...  2.8 us

profile of v6, /device:TPU:0, one launch (start us, length us, event | category | flops | bytes accessed | tf_op | source)
XLA Modules:
  0.0 27.3 jit_solution(12421403753478033945)
XLA Ops:
  0.6 0.0 copy-start
  0.6 23.8 %bev.1 = (bf16[16,4,256]{2,1,0:T(4,128)(2,1)S(1)}, bf16[16,4,128]{2,1,0:T(4,128)(2,1)S(1)}, bf16[192,256]{1,0:T(8,128)(2,1)S(1)}, bf16[32,192,256]{2,1,0:T(8,128...) custom-call(bf16[32,64,256]{2,1,0:T(8,128)(2,1)} %img_hbm.1, ...), custom_call_target="tpu_custom_call" | custom-call | tf_op jit(solution)/shard_map/bev/pallas_call | solution.py:442
  24.4 0.0 copy-done
  24.5 2.8 %back.1 = (bf16[32,64,256]{2,1,0:T(8,128)(2,1)}, bf16[16,4,256]{2,1,0:T(4,128)(2,1)}, bf16[16,4,128]{2,1,0:T(4,128)(2,1)}) custom-call(bf16[2048,256]{1,0:T(8,128)(2,1)S(1)} %get-tuple-element.14.feats, bf16[2048,192]{1,0:T(8,128)(2,1)S(1)} %get-tuple-element.15.amat, f32[2048,128]{1,0:T(8,128)S(1)} %get-tuple-element.16.probs, ...), custom_call_target="tpu_custom_call" | custom-call | tf_op jit(solution)/shard_map/back/pallas_call | solution.py:504
Async XLA Ops:
  0.6 23.8 %copy-start = (bf16[256,118]{0,1:T(8,128)(2,1)S(1)}, bf16[256,118]{0,1:T(8,128)(2,1)}, u32[]{:S(2)}) copy-start(bf16[256,118]{0,1:T(8,128)(2,1)} %param.11) | copy-start | bytes 181252
